TPU v7x, 512 devices: a whole 4x8x8 slice. The times are simulated.
512 devices in a mesh: dp: 8 (over y), ctx: 64 (over z, x, core).
Axes of the slice: x: 4, y: 8, z: 8, core: 2. Of those that a mesh axis runs over, the one named last changes fastest.
Arguments:
- queries: bfloat16 [8, 8192, 1024], P('dp', 'ctx'), may hold values from -6 to 6
- keys: bfloat16 [8, 8192, 1024], P('dp', 'ctx'), may hold values from -0.5390625 to 0.5390625
- values: bfloat16 [8, 8192, 1024], P('dp', 'ctx'), may hold values from -6 to 6
- gain: float32 [1024], replicated, may hold values from 0.1 to 1.9
- grad_out: bfloat16 [8, 8192, 1024], P('dp', 'ctx'), may hold values from -16 to 16
Outputs:
- output: bfloat16 [8, 8192, 1024], P('dp', 'ctx')
- grad_queries: bfloat16 [8, 8192, 1024], P('dp', 'ctx')
- grad_keys: bfloat16 [8, 8192, 1024], P('dp', 'ctx')
- grad_values: bfloat16 [8, 8192, 1024], P('dp', 'ctx')
- grad_gain: float32 [1024], replicated
All inputs are finite; a program needn't handle non-finite values.
Results may differ from a plain program's by a relative error of at most 0.006.
Values sent between devices are 32-bit elements; how exact they have to be, the bound alone decides.
No kernel may reach another device: no remote copies, remote signals or barrier semaphores. Data moves between devices by JAX's collectives and lax.ppermute only.
A program may use at most 128 MiB of HBM per device.

v0:
```python
import jax
import jax.numpy as jnp
from jax import lax
from jax.sharding import PartitionSpec as P

HEAD_DIM = 64
GROUP = 128


def entering(part, axis, combine, identity):
    place = lax.axis_index(axis)
    gathered = lax.all_gather(part, axis)
    state = jnp.zeros_like(part) + jnp.asarray(identity, part.dtype)

    def one(hop, state):
        return combine(state, lax.dynamic_index_in_dim(gathered, hop, 0, False))

    return lax.fori_loop(0, place, one, state)


def add_states(earlier, later_one):
    return earlier + later_one


def per_device(queries, keys, values, gain, grad_out):
    rows = queries.shape[1]
    width = queries.shape[2]
    heads = width // HEAD_DIM
    blocks = rows // GROUP
    shape4 = (blocks, GROUP, heads, HEAD_DIM)
    query_rows = queries.reshape(shape4)
    key_rows = keys.reshape(shape4)
    value_rows = values.reshape(shape4)
    f32 = jnp.float32
    block_kv = jnp.einsum("nrhd,nrhe->nhde", key_rows, value_rows, preferred_element_type=f32)
    local_kv = jnp.sum(block_kv, 0)
    empty_state = jnp.zeros((heads, HEAD_DIM, HEAD_DIM), f32)
    carried = entering(local_kv, "ctx", add_states, empty_state)
    state = carried[None] + (jnp.cumsum(block_kv, 0) - block_kv)
    state_low = state.astype(jnp.bfloat16)
    causal = jnp.tril(jnp.ones((GROUP, GROUP), bool))
    scores = jnp.where(
        causal[None, None],
        jnp.einsum("nthd,nshd->nhts", query_rows, key_rows, preferred_element_type=f32),
        0.0,
    ).astype(jnp.bfloat16)
    attn = jnp.einsum("nhts,nshe->nthe", scores, value_rows, preferred_element_type=f32)
    attn = attn + jnp.einsum("nthd,nhde->nthe", query_rows, state_low, preferred_element_type=f32)
    attn = attn.reshape(rows, width)
    inverse_rms = lax.rsqrt(jnp.mean(attn * attn, -1, keepdims=True) + 1e-06)
    normed = attn * inverse_rms
    output = (normed * gain).astype(jnp.bfloat16)
    grad_f = grad_out[0].astype(f32)
    gain_part = jnp.sum(grad_f * normed, 0)
    grad_norm = grad_f * gain
    grad_attn = (
        inverse_rms * (grad_norm - normed * jnp.mean(grad_norm * normed, -1, keepdims=True))
    ).astype(jnp.bfloat16)
    grad_attn = grad_attn.reshape(shape4)
    block_adjoint = jnp.einsum("nthd,nthe->nhde", query_rows, grad_attn, preferred_element_type=f32)
    local_adjoint = jnp.sum(block_adjoint, 0)
    dscores = jnp.where(
        causal[None, None],
        jnp.einsum("nthe,nshe->nhts", grad_attn, value_rows, preferred_element_type=f32),
        0.0,
    ).astype(jnp.bfloat16)
    grad_queries = jnp.einsum("nhts,nshd->nthd", dscores, key_rows, preferred_element_type=f32)
    grad_queries = grad_queries + jnp.einsum(
        "nthe,nhde->nthd", grad_attn, state_low, preferred_element_type=f32
    )
    grad_keys = jnp.einsum("nhts,nthd->nshd", dscores, query_rows, preferred_element_type=f32)
    grad_values = jnp.einsum("nhts,nthe->nshe", scores, grad_attn, preferred_element_type=f32)
    total, gain_ctx = lax.psum((local_adjoint, gain_part), "ctx")
    before = entering(local_adjoint, "ctx", add_states, empty_state)
    from_later = total - before - local_adjoint
    grad_gain = lax.psum(gain_ctx, "dp")
    from_end = jnp.cumsum(block_adjoint[::-1], 0)[::-1]
    later = from_later[None] + (from_end - block_adjoint)
    later_low = later.astype(jnp.bfloat16)
    grad_keys = grad_keys + jnp.einsum(
        "nshe,nhde->nshd", value_rows, later_low, preferred_element_type=f32
    )
    grad_values = grad_values + jnp.einsum(
        "nshd,nhde->nshe", key_rows, later_low, preferred_element_type=f32
    )
    flat = (1, rows, width)
    return (
        output.reshape(flat),
        grad_queries.reshape(flat).astype(jnp.bfloat16),
        grad_keys.reshape(flat).astype(jnp.bfloat16),
        grad_values.reshape(flat).astype(jnp.bfloat16),
        grad_gain,
    )


def solution(mesh):
    return jax.shard_map(
        per_device,
        mesh=mesh,
        in_specs=(
            P("dp", "ctx", None),
            P("dp", "ctx", None),
            P("dp", "ctx", None),
            P(),
            P("dp", "ctx", None),
        ),
        out_specs=(
            P("dp", "ctx", None),
            P("dp", "ctx", None),
            P("dp", "ctx", None),
            P("dp", "ctx", None),
            P(),
        ),
        check_vma=False,
    )
```

profile of v0, /device:TPU:8, one launch (start us, length us, event | category | flops | bytes accessed | tf_op | source)
XLA Modules:
  0.0 591.7 jit_solution(8018616743634753172)
XLA Ops:
  7.2 1.1 copy.48
  8.3 1.1 copy.49
  9.5 1.1 fusion.22
  10.6 0.8 mul.110
  11.4 1.1 copy.47
  12.5 1.1 copy.52
  13.6 0.4 fusion
  14.0 0.4 convolution_bitcast_fusion.3
  14.4 150.3 %all-gather.5.cloned.1.call-done = f32[1024,64,64]{2,1,0:T(8,128)} async-done(((f32[16,64,64]{2,1,0:T(8,128)}), f32[1024,64,64]{2,1,0:T(8,128)}) %all-gather.5.cloned.1.call-update) | async-done | bytes 16777232 | tf_op jit(solution)/shard_map/all_gather | solution.py:12
  164.7 1.1 add_convert_fusion.1
  166.4 1.2 fusion.11
  168.0 1.0 copy.55
  169.1 1.0 copy.51
  170.3 0.4 fusion.1
  170.6 0.4 convolution_bitcast_fusion.2
  171.1 0.9 fusion.2
  172.0 1.8 copy.58
  173.8 203.0 %psum.22 = f32[1024]{0:T(1024)S(1)} all-reduce(f32[1024]{0:T(1024)S(1)} %get-tuple-element.76), channel_id=1, replica_groups=mesh['dp'=8,'ctx'=64] {'ctx'}, use_global_device_ids=true, to_apply=%region_8.9 | all-reduce | flops 1024 | bytes 8192 | tf_op jit(solution)/shard_map/psum | solution.py:73
  376.8 16.3 %psum.23 = f32[1024]{0:T(1024)} all-reduce(f32[1024]{0:T(1024)S(1)} %psum.22), channel_id=1, replica_groups=mesh['dp'=8,'ctx'=64] {'dp'}, use_global_device_ids=true, to_apply=%region_9.10 | all-reduce | flops 1024 | bytes 8192 | tf_op jit(solution)/shard_map/psum | solution.py:76
  393.1 1.9 multiply_convert_fusion
  395.9 185.8 %all-reduce.2.cloned.1.call-done = f32[16,64,64]{1,2,0:T(8,128)} async-done(((f32[16,64,64]{1,2,0:T(8,128)}), f32[16,64,64]{1,2,0:T(8,128)}) %all-reduce.2.cloned.1.call-update) | async-done | bytes 262160 | tf_op jit(solution)/shard_map/psum | solution.py:73
  581.6 1.3 add_convert_fusion
  583.5 0.8 copy.59
  584.3 0.8 copy.60
  (25 shorter events, 2.6 us)
Async XLA Ops:
  7.2 157.5 %all-gather.5.cloned.1.call-start = ((), (), s32[]{:S(2)}) async-start(), calls=%async_computation.1 | async-start | bytes 34078720 | tf_op jit(solution)/shard_map/all_gather | solution.py:12
  10.6 385.0 %all-gather.7.cloned.1.call-start = ((), (), s32[]{:S(2)}) async-start(), calls=%async_computation.2 | async-start | bytes 34078720 | tf_op jit(solution)/shard_map/all_gather | solution.py:12
  168.0 227.6 %copy-start = (f32[16,64,64]{1,2,0:T(8,128)}, f32[16,64,64]{1,2,0:T(8,128)S(1)}, u32[]{:S(2)}) copy-start(f32[16,64,64]{1,2,0:T(8,128)S(1)} %convolution_bitcast_fusion.1) | copy-start | bytes 786436
  169.0 412.6 %all-reduce.2.cloned.1.call-start = ((), (), s32[]{:S(2)}) async-start(), calls=%async_computation | async-start | bytes 1048576 | tf_op jit(solution)/shard_map/psum | solution.py:73
Sparse Core Ops, SparseCore 0:
  11.4 153.2 all-gather.4
  169.1 219.1 all-gather.6
  395.7 185.8 all-reduce.1
where the time goes:
time: 598 us; the launch traced here: 592 us
  waiting for transfers between devices  336 us (56%)
  blocking collectives  219 us (37%)
  between operations  13.9 us (2%)
  local copies, waits for them, and re-layouts  11.2 us (2%)
    psum x1, blocking collectives, per_device(): total, gain_ctx = lax.psum((local_adjoint, gain_part), 'ctx')  203 us
    psum x1, waiting for transfers between devices, per_device(): total, gain_ctx = lax.psum((local_adjoint, gain_part), 'ctx')  186 us
    all_gather x2, waiting for transfers between devices, entering(): gathered = lax.all_gather(part, axis)  150 us
    psum x1, blocking collectives, per_device(): grad_gain = lax.psum(gain_ctx, 'dp')  16.3 us
  transfers between devices with their start and end apart: 3, of which 2 were waited for; matrix products, arithmetic and copies ran while one was open for 2% of the time, Pallas kernels for 0%

commit v1 on v0

v1 whole, which is shorter than its diff:
```python
import jax
import jax.numpy as jnp
from jax import lax
from jax.experimental import pallas as pl
from jax.experimental.pallas import tpu as pltpu
from jax.sharding import PartitionSpec as P

HEAD_DIM = 64
PAIR = 2 * HEAD_DIM
F32 = jnp.float32
BF16 = jnp.bfloat16
VMEM = pl.BlockSpec(memory_space=pltpu.VMEM)


def mm(a, b):
    return lax.dot_general(a, b, (((1,), (0,)), ((), ())), preferred_element_type=F32)


def mm_bt(a, b):
    return lax.dot_general(a, b, (((1,), (1,)), ((), ())), preferred_element_type=F32)


def mm_at(a, b):
    return lax.dot_general(a, b, (((0,), (0,)), ((), ())), preferred_element_type=F32)


def halves():
    lane = lax.broadcasted_iota(jnp.int32, (1, PAIR), 1)
    first = jnp.where(lane < HEAD_DIM, 1.0, 0.0).astype(BF16)
    second = jnp.where(lane < HEAD_DIM, 0.0, 1.0).astype(BF16)
    return first, second


def stack(x, masks):
    return jnp.concatenate([x * masks[0], x * masks[1]], axis=0)


def pack(full):
    lane = lax.broadcasted_iota(jnp.int32, (HEAD_DIM, PAIR), 1)
    return jnp.where(lane < HEAD_DIM, full[:HEAD_DIM], full[HEAD_DIM:])


def cols(p):
    return slice(p * PAIR, (p + 1) * PAIR)


def kv_kernel(k_ref, v_ref, kv_ref):
    for p in range(kv_ref.shape[0]):
        kv_ref[p] = pack(mm_at(k_ref[:, cols(p)], v_ref[:, cols(p)]))


def scores_kernel(q_ref, k_ref, v_ref, intra_ref):
    rows = q_ref.shape[0]
    masks = halves()
    t = lax.broadcasted_iota(jnp.int32, (rows, rows), 0)
    s = lax.broadcasted_iota(jnp.int32, (rows, rows), 1)
    causal = s <= t
    for p in range(q_ref.shape[1] // PAIR):
        q, k, v = q_ref[:, cols(p)], k_ref[:, cols(p)], v_ref[:, cols(p)]
        sc = mm_bt(stack(q, masks), k)
        sc = jnp.concatenate(
            [jnp.where(causal, sc[:rows], 0.0).astype(BF16), jnp.where(causal, sc[rows:], 0.0).astype(BF16)],
            axis=1,
        )
        intra_ref[:, cols(p)] = mm(sc, stack(v, masks))


def attn_kernel(state_ref, q_ref, intra_ref, gain_ref, g_ref, out_ref, ga_ref, sent_ref, attn_ref, gg_ref):
    rows, width = q_ref.shape
    pairs = width // PAIR
    part = sent_ref.shape[1] - pairs
    masks = halves()
    square = jnp.zeros((rows, PAIR), F32)
    for p in range(pairs):
        low = state_ref[p].astype(BF16)
        attn = intra_ref[:, cols(p)] + mm(q_ref[:, cols(p)], stack(low, masks))
        attn_ref[:, cols(p)] = attn
        square = square + attn * attn
    inv = lax.rsqrt(jnp.sum(square, 1, keepdims=True) * (1.0 / width) + 1e-06)
    dots = jnp.zeros((rows, PAIR), F32)
    for p in range(pairs):
        normed = attn_ref[:, cols(p)] * inv
        attn_ref[:, cols(p)] = normed
        gain = gain_ref[:, cols(p)]
        out_ref[:, cols(p)] = (normed * gain).astype(BF16)
        gn = g_ref[:, cols(p)].astype(F32) * normed
        gg_ref[p : p + 1, :] = jnp.sum(gn, 0, keepdims=True)
        dots = dots + gn * gain
    mean = jnp.sum(dots, 1, keepdims=True) * (1.0 / width)
    for p in range(pairs):
        dn = g_ref[:, cols(p)].astype(F32) * gain_ref[:, cols(p)]
        ga = (inv * (dn - attn_ref[:, cols(p)] * mean)).astype(BF16)
        ga_ref[:, cols(p)] = ga
        per = HEAD_DIM // part
        sent_ref[per * p : per * (p + 1), :part, :] = pack(mm_at(q_ref[:, cols(p)], ga)).reshape(per, part, PAIR)
    own = gg_ref[...]
    for i in range(sent_ref.shape[0]):
        sent_ref[i, part:, :] = own


def local_kernel(state_ref, q_ref, k_ref, v_ref, ga_ref, gq_ref, gk_ref, gv_ref):
    rows = q_ref.shape[0]
    masks = halves()
    t = lax.broadcasted_iota(jnp.int32, (rows, rows), 0)
    s = lax.broadcasted_iota(jnp.int32, (rows, rows), 1)
    causal = s <= t
    causal_t = t <= s

    def both(x, mask):
        return jnp.where(mask, x, 0.0).astype(BF16)

    for p in range(q_ref.shape[1] // PAIR):
        q, k, v, ga = q_ref[:, cols(p)], k_ref[:, cols(p)], v_ref[:, cols(p)], ga_ref[:, cols(p)]
        low = state_ref[p].astype(BF16)
        ga2, q2 = stack(ga, masks), stack(q, masks)
        ds = mm_bt(ga2, v)
        ds = jnp.concatenate([both(ds[:rows], causal), both(ds[rows:], causal)], axis=1)
        gq = mm(ds, stack(k, masks)) + mm_bt(ga, stack(low, masks))
        gq_ref[:, cols(p)] = gq.astype(BF16)
        dst = mm_bt(v, ga2)
        dst = jnp.concatenate([both(dst[:, :rows], causal_t), both(dst[:, rows:], causal_t)], axis=1)
        gk_ref[:, cols(p)] = mm(dst, q2)
        sct = mm_bt(k, q2)
        sct = jnp.concatenate([both(sct[:, :rows], causal_t), both(sct[:, rows:], causal_t)], axis=1)
        gv_ref[:, cols(p)] = mm(sct, ga2)


def later_kernel(later_ref, k_ref, v_ref, gk_ref, gv_ref, gk_out, gv_out):
    masks = halves()
    for p in range(k_ref.shape[1] // PAIR):
        low = stack(later_ref[p].astype(BF16), masks)
        gk_out[:, cols(p)] = (gk_ref[:, cols(p)] + mm_bt(v_ref[:, cols(p)], low)).astype(BF16)
        gv_out[:, cols(p)] = (gv_ref[:, cols(p)] + mm(k_ref[:, cols(p)], low)).astype(BF16)


def prefix_kernel(x_ref, o_ref):
    acc = jnp.zeros(o_ref.shape[1:], F32)
    for i in range(x_ref.shape[0]):
        o_ref[i] = acc
        acc = acc + x_ref[i]


def suffix_kernel(x_ref, o_ref, gg_ref):
    part = o_ref.shape[1]
    total = jnp.zeros(gg_ref.shape, F32)
    acc = jnp.zeros(o_ref.shape[1:], F32)
    for i in reversed(range(x_ref.shape[0])):
        o_ref[i] = acc
        acc = acc + x_ref[i, :part, :]
        total = total + x_ref[i, part:, :]
    gg_ref[...] = total


def call(kernel, outs, args, name, flops, scratch=(), near=None):
    moved = sum(a.size * a.dtype.itemsize for a in args) + sum(o.size * o.dtype.itemsize for o in outs)
    near = (True,) * len(outs) if near is None else near
    shapes = tuple(pltpu.VMEM(o.shape, o.dtype) if n else o for o, n in zip(outs, near))
    single = len(outs) == 1
    return pl.pallas_call(
        kernel,
        out_shape=shapes[0] if single else shapes,
        in_specs=[VMEM] * len(args),
        out_specs=VMEM if single else (VMEM,) * len(outs),
        scratch_shapes=list(scratch),
        compiler_params=pltpu.CompilerParams(vmem_limit_bytes=16 * 1024 * 1024),
        cost_estimate=pl.CostEstimate(flops=flops, bytes_accessed=moved, transcendentals=0),
        name=name,
    )(*(pltpu.with_memory_space_constraint(a, pltpu.VMEM) for a in args))


def exchange(x):
    return lax.all_to_all(x, "ctx", 0, 0, tiled=True)


def make(ctx):
    def per_device(queries, keys, values, gain, grad_out):
        _, rows, width = queries.shape
        pairs = width // PAIR
        q, k, v, g = (x.reshape(rows, width) for x in (queries, keys, values, grad_out))
        gain = gain.reshape(1, width)
        sds = jax.ShapeDtypeStruct
        part = pairs * HEAD_DIM // ctx
        piece = (ctx, part, PAIR)
        state_shape = (pairs, HEAD_DIM, PAIR)
        flops = 2 * rows * rows * width

        kv = call(kv_kernel, (sds(state_shape, F32),), (k, v), "kv", flops)
        sent = exchange(kv.reshape(piece))
        intra = call(scores_kernel, (sds((rows, width), F32),), (q, k, v), "scores", 4 * flops)
        before = call(prefix_kernel, (sds(piece, F32),), (sent,), "prefix", 0)
        state = exchange(before).reshape(state_shape)
        out, ga, sent = call(
            attn_kernel,
            (sds((rows, width), BF16), sds((rows, width), BF16), sds((ctx, part + pairs, PAIR), F32)),
            (state, q, intra, gain, g),
            "attn",
            2 * flops,
            scratch=(pltpu.VMEM((rows, width), F32), pltpu.VMEM((pairs, PAIR), F32)),
            near=(False, True, False),
        )
        sent = exchange(sent)
        gq, gk, gv = call(
            local_kernel,
            (sds((rows, width), BF16), sds((rows, width), F32), sds((rows, width), F32)),
            (state, q, k, v, ga),
            "local",
            10 * flops,
            near=(False, True, True),
        )
        sent, gk, gv = lax.optimization_barrier((sent, gk, gv))
        after, gg = call(suffix_kernel, (sds(piece, F32), sds((pairs, PAIR), F32)), (sent,), "suffix", 0, near=(False, True))
        later = exchange(after).reshape(state_shape)
        gg = lax.psum(gg, "dp")
        later, gg = lax.optimization_barrier((later, gg))
        gk, gv = call(
            later_kernel,
            (sds((rows, width), BF16), sds((rows, width), BF16)),
            (later, k, v, gk, gv),
            "later",
            2 * flops,
            near=(False, False),
        )
        flat = (1, rows, width)
        return out.reshape(flat), gq.reshape(flat), gk.reshape(flat), gv.reshape(flat), gg.reshape(width)

    return per_device


def solution(mesh):
    seq = P("dp", "ctx", None)
    return jax.shard_map(
        make(mesh.shape["ctx"]),
        mesh=mesh,
        in_specs=(seq, seq, seq, P(), seq),
        out_specs=(seq, seq, seq, seq, P()),
        check_vma=False,
    )
```

time: 598 us -> 98.7 us (0.17)
  the two profiles are of different devices: /device:TPU:8 before, /device:TPU:2 now
where the time goes in v1:
time: 98.7 us; the launch traced here: 98.3 us
  blocking collectives  44.1 us (45%)
  waiting for transfers between devices  26.9 us (27%)
  starting transfers between devices  17.3 us (18%)
  Pallas kernels  7.36 us (7%)
  local copies, waits for them, and re-layouts  1.92 us (2%)
    all_to_all x3, waiting for transfers between devices, exchange(): return lax.all_to_all(x, 'ctx', 0, 0, tiled=True)  26.9 us
    all_to_all x1, blocking collectives, exchange(): return lax.all_to_all(x, 'ctx', 0, 0, tiled=True)  25.9 us
    psum x1, blocking collectives, per_device(): gg = lax.psum(gg, 'dp')  18.2 us
    all_to_all x3, starting transfers between devices, exchange(): return lax.all_to_all(x, 'ctx', 0, 0, tiled=True)  17.3 us
    pallas_call x7, Pallas kernels, call(): pl.pallas_call(kernel, out_shape=shapes[0] if single else shapes, in_spec...  7.36 us
  transfers between devices with their start and end apart: 3, of which 2 were waited for; matrix products, arithmetic and copies ran while one was open for 0% of the time, Pallas kernels for 3%

profile of v1, /device:TPU:2, one launch (start us, length us, event | category | flops | bytes accessed | tf_op | source)
XLA Modules:
  0.0 98.3 jit_solution(6612889951083518671)
XLA Ops:
  0.6 0.0 copy-start
  0.6 0.9 copy-done
  1.6 0.9 copy-done.2
  2.5 0.3 kv.1
  2.8 25.9 %all_to_all.20.x_ref = f32[64,8,128]{2,1,0:T(8,128)S(1)} all-to-all(f32[64,8,128]{2,1,0:T(8,128)S(1)} %bitcast.27), channel_id=1, replica_groups=mesh['dp'=8,'ctx'=64] {'ctx'}, dimensions={0} | all-to-all | bytes 524288 | tf_op jit(solution)/shard_map/all_to_all | solution.py:172
  28.7 0.8 prefix.1
  29.5 5.8 %all-to-all-start.1 = ((f32[64,8,128]{2,1,0:T(8,128)}), f32[64,8,128]{2,1,0:T(8,128)S(1)}, u32[]{:S(2)}, u32[]{:S(2)}) async-start(f32[64,8,128]{2,1,0:T(8,128)} %prefix.1), calls=%async_computation.1 | async-start | bytes 524288 | tf_op jit(solution)/shard_map/all_to_all | solution.py:172
  35.2 0.0 copy-done.4
  35.3 0.0 copy-done.1
  35.3 0.0 copy-done.3
  35.3 0.0 copy-start.5
  35.3 0.7 scores.1.intra_ref
  36.0 0.0 copy-start.6
  36.0 11.5 %all-to-all-done.1 = f32[64,8,128]{2,1,0:T(8,128)S(1)} async-done(((f32[64,8,128]{2,1,0:T(8,128)}), f32[64,8,128]{2,1,0:T(8,128)S(1)}, u32[]{:S(2)}, u32[]{:S(2)}) %all-to-all-start.1) | async-done | bytes 262176 | tf_op jit(solution)/shard_map/all_to_all | solution.py:172
  47.5 0.0 copy-done.5
  47.5 1.6 %attn.1 = (bf16[128,1024]{1,0:T(8,128)(2,1)}, bf16[128,1024]{1,0:T(8,128)(2,1)S(1)}, f32[64,16,128]{2,1,0:T(8,128)}) custom-call(f32[8,64,128]{2,1,0:T(8,128)S(1)} %bitcast.24, bf16[128,1024]{1,0:T(8,128)(2,1)S(1)} %bitcast.22, f32[128,1024]{1,0:T(8,128)S(1)} %scores.1.intra_ref, f32[1,1024]{1,0:T(1,128)S(1)} %bitcast.29, bf16[128,1024]{1,0:T(8,128)(2,1)S(1)} %bitcast.28), custom_call_target="tpu_custom_call" | custom-call | flops 67108864 | bytes 2363392 | tf_op jit(solution)/shard_map/attn/pallas_call | solution.py:159
  49.0 5.7 %all-to-all-start.2 = ((f32[64,16,128]{2,1,0:T(8,128)}), f32[64,16,128]{2,1,0:T(8,128)S(1)}, u32[]{:S(2)}, u32[]{:S(2)}) async-start(f32[64,16,128]{2,1,0:T(8,128)} %get-tuple-element.23), calls=%async_computation.2 | async-start | bytes 1048576 | tf_op jit(solution)/shard_map/all_to_all | solution.py:172
  54.7 2.2 %local.1 = (bf16[128,1024]{1,0:T(8,128)(2,1)}, f32[128,1024]{1,0:T(8,128)S(1)}, f32[128,1024]{1,0:T(8,128)S(1)}) custom-call(f32[8,64,128]{2,1,0:T(8,128)S(1)} %bitcast.25, bf16[128,1024]{1,0:T(8,128)(2,1)S(1)} %bitcast.23, bf16[128,1024]{1,0:T(8,128)(2,1)S(1)} %bitcast.15, bf16[128,1024]{1,0:T(8,128)(2,1)S(1)} %bitcast.19, ...), custom_call_target="tpu_custom_call" | custom-call | flops 335544320 | bytes 2621440 | tf_op jit(solution)/shard_map/local/pallas_call | solution.py:159
  56.9 15.4 %all-to-all-done.2.x_ref = f32[64,16,128]{2,1,0:T(8,128)S(1)} async-done(((f32[64,16,128]{2,1,0:T(8,128)}), f32[64,16,128]{2,1,0:T(8,128)S(1)}, u32[]{:S(2)}, u32[]{:S(2)}) %all-to-all-start.2) | async-done | bytes 524320 | tf_op jit(solution)/shard_map/all_to_all | solution.py:172
  72.3 0.8 suffix.1
  73.0 5.9 %all-to-all-start.3 = ((f32[64,8,128]{2,1,0:T(8,128)}), f32[64,8,128]{2,1,0:T(8,128)S(1)}, u32[]{:S(2)}, u32[]{:S(2)}) async-start(f32[64,8,128]{2,1,0:T(8,128)} %get-tuple-element.27), calls=%async_computation.3 | async-start | bytes 524288 | tf_op jit(solution)/shard_map/all_to_all | solution.py:172
  78.9 18.2 %psum.7 = f32[8,128]{1,0:T(8,128)} all-reduce(f32[8,128]{1,0:T(8,128)S(1)} %get-tuple-element.28), channel_id=1, replica_groups=mesh['dp'=8,'ctx'=64] {'dp'}, use_global_device_ids=true, to_apply=%region_0.0 | all-reduce | flops 1024 | bytes 8192 | tf_op jit(solution)/shard_map/psum | solution.py:213
  97.1 0.0 all-to-all-done.3
  97.1 1.2 %later.1 = (bf16[128,1024]{1,0:T(8,128)(2,1)}, bf16[128,1024]{1,0:T(8,128)(2,1)}) custom-call(f32[8,64,128]{2,1,0:T(8,128)S(1)} %bitcast.26, bf16[128,1024]{1,0:T(8,128)(2,1)S(1)} %bitcast.16, bf16[128,1024]{1,0:T(8,128)(2,1)S(1)} %bitcast.20, f32[128,1024]{1,0:T(8,128)S(1)} %get-tuple-element.30.gk_ref, f32[128,1024]{1,0:T(8,128)S(1)} %get-tuple-element.31.gv_ref), custom_call_target="tpu_custom_call" | custom-call | flops 67108864 | bytes 2359296 | tf_op jit(solution)/shard_map/later/pallas_call | solution.py:159
  (5 shorter events, 0.0 us)
Async XLA Ops:
  0.6 1.0 copy-start
  1.6 0.9 copy-start.2
  28.7 6.6 %copy-start.4 = (bf16[1,128,1024]{2,1,0:T(8,128)(2,1)S(1)}, bf16[1,128,1024]{2,1,0:T(8,128)(2,1)}, u32[]{:S(2)}) copy-start(bf16[1,128,1024]{2,1,0:T(8,128)(2,1)} %param.5) | copy-start | bytes 786436
  29.4 5.8 %copy-start.1 = (bf16[1,128,1024]{2,1,0:T(8,128)(2,1)S(1)}, bf16[1,128,1024]{2,1,0:T(8,128)(2,1)}, u32[]{:S(2)}) copy-start(bf16[1,128,1024]{2,1,0:T(8,128)(2,1)} %param.6) | copy-start | bytes 786436
  29.5 5.8 %copy-start.3 = (bf16[1,128,1024]{2,1,0:T(8,128)(2,1)S(1)}, bf16[1,128,1024]{2,1,0:T(8,128)(2,1)}, u32[]{:S(2)}) copy-start(bf16[1,128,1024]{2,1,0:T(8,128)(2,1)} %param.7) | copy-start | bytes 786436
  29.5 18.0 %all-to-all-start.1 = ((f32[64,8,128]{2,1,0:T(8,128)}), f32[64,8,128]{2,1,0:T(8,128)S(1)}, u32[]{:S(2)}, u32[]{:S(2)}) async-start(f32[64,8,128]{2,1,0:T(8,128)} %prefix.1), calls=%async_computation.1 | async-start | bytes 524288 | tf_op jit(solution)/shard_map/all_to_all | solution.py:172
  35.3 12.2 %copy-start.5 = (bf16[1,128,1024]{2,1,0:T(8,128)(2,1)S(1)}, bf16[1,128,1024]{2,1,0:T(8,128)(2,1)}, u32[]{:S(2)}) copy-start(bf16[1,128,1024]{2,1,0:T(8,128)(2,1)} %param.9) | copy-start | bytes 786436
  36.0 11.5 %copy-start.6 = (f32[1024]{0:T(1024)S(1)}, f32[1024]{0:T(1024)}, u32[]{:S(2)}) copy-start(f32[1024]{0:T(1024)} %param.8) | copy-start | bytes 12292
  49.0 23.2 %all-to-all-start.2 = ((f32[64,16,128]{2,1,0:T(8,128)}), f32[64,16,128]{2,1,0:T(8,128)S(1)}, u32[]{:S(2)}, u32[]{:S(2)}) async-start(f32[64,16,128]{2,1,0:T(8,128)} %get-tuple-element.23), calls=%async_computation.2 | async-start | bytes 1048576 | tf_op jit(solution)/shard_map/all_to_all | solution.py:172
  73.0 24.1 %all-to-all-start.3 = ((f32[64,8,128]{2,1,0:T(8,128)}), f32[64,8,128]{2,1,0:T(8,128)S(1)}, u32[]{:S(2)}, u32[]{:S(2)}) async-start(f32[64,8,128]{2,1,0:T(8,128)} %get-tuple-element.27), calls=%async_computation.3 | async-start | bytes 524288 | tf_op jit(solution)/shard_map/all_to_all | solution.py:172

commit v2 on v1

--- a/solution.py
+++ b/solution.py
@@ -1,3 +1,5 @@
+import functools
+
 import jax
 import jax.numpy as jnp
 from jax import lax
@@ -44,12 +46,28 @@
     return slice(p * PAIR, (p + 1) * PAIR)
 
 
-def kv_kernel(k_ref, v_ref, kv_ref):
-    for p in range(kv_ref.shape[0]):
-        kv_ref[p] = pack(mm_at(k_ref[:, cols(p)], v_ref[:, cols(p)]))
-
-
-def scores_kernel(q_ref, k_ref, v_ref, intra_ref):
+def kv_kernel(k_hbm, v_hbm, kv_ref, k_ref, v_ref, sems):
+    chunks = sems.shape[1]
+    wide = k_ref.shape[1] // chunks
+
+    def copies(c):
+        at = slice(c * wide, (c + 1) * wide)
+        return (
+            pltpu.make_async_copy(k_hbm.at[:, at], k_ref.at[:, at], sems.at[0, c]),
+            pltpu.make_async_copy(v_hbm.at[:, at], v_ref.at[:, at], sems.at[1, c]),
+        )
+
+    for c in range(chunks):
+        for copy in copies(c):
+            copy.start()
+    for c in range(chunks):
+        for copy in copies(c):
+            copy.wait()
+        for p in range(c * wide // PAIR, (c + 1) * wide // PAIR):
+            kv_ref[p] = pack(mm_at(k_ref[:, cols(p)], v_ref[:, cols(p)]))
+
+
+def scores_kernel(q_ref, k_ref, v_ref, gain_ref, intra_ref, gain_out):
     rows = q_ref.shape[0]
     masks = halves()
     t = lax.broadcasted_iota(jnp.int32, (rows, rows), 0)
@@ -63,12 +81,14 @@
             axis=1,
         )
         intra_ref[:, cols(p)] = mm(sc, stack(v, masks))
+    gain_out[...] = gain_ref[...]
 
 
 def attn_kernel(state_ref, q_ref, intra_ref, gain_ref, g_ref, out_ref, ga_ref, sent_ref, attn_ref, gg_ref):
     rows, width = q_ref.shape
     pairs = width // PAIR
     part = sent_ref.shape[1] - pairs
+    per = HEAD_DIM // part
     masks = halves()
     square = jnp.zeros((rows, PAIR), F32)
     for p in range(pairs):
@@ -91,7 +111,6 @@
         dn = g_ref[:, cols(p)].astype(F32) * gain_ref[:, cols(p)]
         ga = (inv * (dn - attn_ref[:, cols(p)] * mean)).astype(BF16)
         ga_ref[:, cols(p)] = ga
-        per = HEAD_DIM // part
         sent_ref[per * p : per * (p + 1), :part, :] = pack(mm_at(q_ref[:, cols(p)], ga)).reshape(per, part, PAIR)
     own = gg_ref[...]
     for i in range(sent_ref.shape[0]):
@@ -133,65 +152,99 @@
         gv_out[:, cols(p)] = (gv_ref[:, cols(p)] + mm(k_ref[:, cols(p)], low)).astype(BF16)
 
 
-def prefix_kernel(x_ref, o_ref):
+def total_kernel(x_ref, o_ref):
+    total = x_ref[0]
+    for i in range(1, x_ref.shape[0]):
+        total = total + x_ref[i]
+    o_ref[...] = total
+
+
+def earlier_kernel(x_ref, *refs):
+    outside, o_ref = refs[:-1], refs[-1]
     acc = jnp.zeros(o_ref.shape[1:], F32)
+    for ref in outside:
+        acc = acc + ref[...]
     for i in range(x_ref.shape[0]):
         o_ref[i] = acc
         acc = acc + x_ref[i]
 
 
-def suffix_kernel(x_ref, o_ref, gg_ref):
+def later_sums_kernel(x_ref, o_ref, gg_ref):
     part = o_ref.shape[1]
-    total = jnp.zeros(gg_ref.shape, F32)
-    acc = jnp.zeros(o_ref.shape[1:], F32)
+    acc = jnp.zeros((part, PAIR), F32)
+    gain = jnp.zeros(gg_ref.shape, F32)
     for i in reversed(range(x_ref.shape[0])):
         o_ref[i] = acc
         acc = acc + x_ref[i, :part, :]
-        total = total + x_ref[i, part:, :]
-    gg_ref[...] = total
-
-
-def call(kernel, outs, args, name, flops, scratch=(), near=None):
+        gain = gain + x_ref[i, part:, :]
+    gg_ref[...] = gain
+
+
+def call(kernel, outs, args, name, flops, scratch=(), near=None, far=False):
     moved = sum(a.size * a.dtype.itemsize for a in args) + sum(o.size * o.dtype.itemsize for o in outs)
     near = (True,) * len(outs) if near is None else near
     shapes = tuple(pltpu.VMEM(o.shape, o.dtype) if n else o for o, n in zip(outs, near))
     single = len(outs) == 1
+    space = pltpu.HBM if far else pltpu.VMEM
     return pl.pallas_call(
         kernel,
         out_shape=shapes[0] if single else shapes,
-        in_specs=[VMEM] * len(args),
+        in_specs=[pl.BlockSpec(memory_space=space)] * len(args),
         out_specs=VMEM if single else (VMEM,) * len(outs),
         scratch_shapes=list(scratch),
         compiler_params=pltpu.CompilerParams(vmem_limit_bytes=16 * 1024 * 1024),
         cost_estimate=pl.CostEstimate(flops=flops, bytes_accessed=moved, transcendentals=0),
         name=name,
-    )(*(pltpu.with_memory_space_constraint(a, pltpu.VMEM) for a in args))
-
-
-def exchange(x):
-    return lax.all_to_all(x, "ctx", 0, 0, tiled=True)
-
-
-def make(ctx):
+    )(*(pltpu.with_memory_space_constraint(a, space) for a in args))
+
+
+def make(ctx, members):
+    groups = ctx // members
+    inside = [[g * members + r for r in range(members)] for g in range(groups)]
+
+    def exchange(x, devices=None):
+        return lax.all_to_all(x, "ctx", 0, 0, tiled=True, axis_index_groups=devices)
+
+    def from_earlier(total):
+        return [
+            lax.ppermute(total, "ctx", [(i, i + d * members) for i in range(ctx - d * members)])
+            for d in range(1, groups)
+        ]
+
     def per_device(queries, keys, values, gain, grad_out):
         _, rows, width = queries.shape
         pairs = width // PAIR
         q, k, v, g = (x.reshape(rows, width) for x in (queries, keys, values, grad_out))
         gain = gain.reshape(1, width)
         sds = jax.ShapeDtypeStruct
-        part = pairs * HEAD_DIM // ctx
-        piece = (ctx, part, PAIR)
+        part = pairs * HEAD_DIM // members
+        piece = (members, part, PAIR)
+        small = pairs * HEAD_DIM // ctx
         state_shape = (pairs, HEAD_DIM, PAIR)
         flops = 2 * rows * rows * width
 
-        kv = call(kv_kernel, (sds(state_shape, F32),), (k, v), "kv", flops)
-        sent = exchange(kv.reshape(piece))
-        intra = call(scores_kernel, (sds((rows, width), F32),), (q, k, v), "scores", 4 * flops)
-        before = call(prefix_kernel, (sds(piece, F32),), (sent,), "prefix", 0)
-        state = exchange(before).reshape(state_shape)
+        tile = sds((rows, width), BF16)
+        kv, k, v = call(
+            kv_kernel,
+            (sds(state_shape, F32), tile, tile),
+            (k, v),
+            "kv",
+            flops,
+            scratch=(pltpu.SemaphoreType.DMA((2, 4)),),
+            far=True,
+        )
+        sent = exchange(kv.reshape(piece), inside)
+        total = call(total_kernel, (sds((part, PAIR), F32),), (sent,), "total", 0)
+        outside = from_earlier(total)
+        intra, gain = call(
+            scores_kernel, (sds((rows, width), F32), sds((1, width), F32)), (q, k, v, gain), "scores", 4 * flops
+        )
+        sent, intra, *outside = lax.optimization_barrier((sent, intra, *outside))
+        before = call(earlier_kernel, (sds(piece, F32),), (sent, *outside), "earlier", 0)
+        state = exchange(before, inside).reshape(state_shape)
         out, ga, sent = call(
             attn_kernel,
-            (sds((rows, width), BF16), sds((rows, width), BF16), sds((ctx, part + pairs, PAIR), F32)),
+            (sds((rows, width), BF16), sds((rows, width), BF16), sds((ctx, small + pairs, PAIR), F32)),
             (state, q, intra, gain, g),
             "attn",
             2 * flops,
@@ -208,7 +261,14 @@
             near=(False, True, True),
         )
         sent, gk, gv = lax.optimization_barrier((sent, gk, gv))
-        after, gg = call(suffix_kernel, (sds(piece, F32), sds((pairs, PAIR), F32)), (sent,), "suffix", 0, near=(False, True))
+        after, gg = call(
+            later_sums_kernel,
+            (sds((ctx, small, PAIR), F32), sds((pairs, PAIR), F32)),
+            (sent,),
+            "later_sums",
+            0,
+            near=(False, True),
+        )
         later = exchange(after).reshape(state_shape)
         gg = lax.psum(gg, "dp")
         later, gg = lax.optimization_barrier((later, gg))
@@ -229,7 +289,7 @@
 def solution(mesh):
     seq = P("dp", "ctx", None)
     return jax.shard_map(
-        make(mesh.shape["ctx"]),
+        make(mesh.shape["ctx"], 16),
         mesh=mesh,
         in_specs=(seq, seq, seq, P(), seq),
         out_specs=(seq, seq, seq, seq, P()),

time: 98.7 us -> 96.7 us (0.980)
  starting transfers between devices: 17.3 us -> 28.4 us
  waiting for transfers between devices: 26.9 us -> 16.1 us
  local copies, waits for them, and re-layouts: 1.92 us -> 0.02 us
  blocking collectives: 44.1 us -> 42.8 us
    ppermute x0 -> x3, starting transfers between devices: none -> 13.8 us  [from_earlier(): lax.ppermute(total, 'ctx', [(i, i + d * members) for i in range(ctx - d *...]
    all_to_all x3 -> x2, waiting for transfers between devices: 26.9 us -> 15.4 us  [exchange(): return lax.all_to_all(x, 'ctx', 0, 0, tiled=True, axis_index_groups=devices)]
    all_to_all x3 -> x2, starting transfers between devices: 17.3 us -> 14.7 us  [exchange(): return lax.all_to_all(x, 'ctx', 0, 0, tiled=True, axis_index_groups=devices)]
    unnamed x14 -> x6, local copies, waits for them, and re-layouts: 1.92 us -> 0.02 us
    all_to_all x1 -> x2, blocking collectives: 25.9 us -> 24.6 us  [exchange(): return lax.all_to_all(x, 'ctx', 0, 0, tiled=True, axis_index_groups=devices)]
    pallas_call x7 -> x8, Pallas kernels: 7.36 us -> 8.13 us  [call(): pl.pallas_call(kernel, out_shape=shapes[0] if single else shapes, in_spec...]
  transfers between devices with their start and end apart: 3 -> 5, of which waited for: 2 -> 2; matrix products, arithmetic and copies ran while one was open for 0% -> 0% of each run, Pallas kernels for 3% -> 3%
where the time goes in v2:
time: 96.7 us; the launch traced here: 96.3 us
  blocking collectives  42.8 us (44%)
  starting transfers between devices  28.4 us (29%)
  waiting for transfers between devices  16.1 us (17%)
  Pallas kernels  8.13 us (8%)
    all_to_all x2, blocking collectives, exchange(): return lax.all_to_all(x, 'ctx', 0, 0, tiled=True, axis_index_groups=devices)  24.6 us
    psum x1, blocking collectives, per_device(): gg = lax.psum(gg, 'dp')  18.2 us
    all_to_all x2, waiting for transfers between devices, exchange(): return lax.all_to_all(x, 'ctx', 0, 0, tiled=True, axis_index_groups=devices)  15.4 us
    all_to_all x2, starting transfers between devices, exchange(): return lax.all_to_all(x, 'ctx', 0, 0, tiled=True, axis_index_groups=devices)  14.7 us
    ppermute x3, starting transfers between devices, from_earlier(): lax.ppermute(total, 'ctx', [(i, i + d * members) for i in range(ctx - d *...  13.8 us
    pallas_call x8, Pallas kernels, call(): pl.pallas_call(kernel, out_shape=shapes[0] if single else shapes, in_spec...  8.13 us
  transfers between devices with their start and end apart: 5, of which 2 were waited for; matrix products, arithmetic and copies ran while one was open for 0% of the time, Pallas kernels for 3%

profile of v2, /device:TPU:2, one launch (start us, length us, event | category | flops | bytes accessed | tf_op | source)
XLA Modules:
  0.0 96.3 jit_solution(5512108332206686535)
XLA Ops:
  0.6 1.7 %kv.1 = (f32[8,64,128]{2,1,0:T(8,128)S(1)}, bf16[128,1024]{1,0:T(8,128)(2,1)S(1)}, bf16[128,1024]{1,0:T(8,128)(2,1)S(1)}) custom-call(bf16[128,1024]{1,0:T(8,128)(2,1)} %bitcast.22, bf16[128,1024]{1,0:T(8,128)(2,1)} %bitcast.23), custom_call_target="tpu_custom_call" | custom-call | flops 33554432 | bytes 1310720 | tf_op jit(solution)/shard_map/kv/pallas_call | solution.py:189
  2.4 13.9 %all_to_all.20.x_ref = f32[16,32,128]{2,1,0:T(8,128)S(1)} all-to-all(f32[16,32,128]{2,1,0:T(8,128)S(1)} %bitcast.20), channel_id=1, replica_groups={{0,1,2,3,4,5,6,7,8,9,10,11,12,13,14,15},{16,17,18,19,20,21,22,23,24,25,..., dimensions={0} | all-to-all | bytes 524288 | tf_op jit(solution)/shard_map/all_to_all | solution.py:206
  16.3 0.0 copy-start.2
  16.3 8.2 %collective-permute-start.2 = (f32[32,128]{1,0:T(8,128)S(1)}, f32[32,128]{1,0:T(8,128)S(1)}, u32[]{:S(2)}, u32[]{:S(2)}) collective-permute-start(f32[32,128]{1,0:T(8,128)S(1)} %total.1), channel_id=1, source_target_pairs={{0,48},{1,49},{2,50},{3,51},{4,52},{5,53},{6,54},{7,55},{8,56},{9,... | collective-permute-start | bytes 49160 | tf_op jit(solution)/shard_map/ppermute | solution.py:210
  24.5 1.3 %collective-permute-start.1 = (f32[32,128]{1,0:T(8,128)S(1)}, f32[32,128]{1,0:T(8,128)S(1)}, u32[]{:S(2)}, u32[]{:S(2)}) collective-permute-start(f32[32,128]{1,0:T(8,128)S(1)} %total.1), channel_id=1, source_target_pairs={{0,32},{1,33},{2,34},{3,35},{4,36},{5,37},{6,38},{7,39},{8,40},{9,... | collective-permute-start | bytes 49160 | tf_op jit(solution)/shard_map/ppermute | solution.py:210
  25.8 4.3 %collective-permute-start = (f32[32,128]{1,0:T(8,128)S(1)}, f32[32,128]{1,0:T(8,128)S(1)}, u32[]{:S(2)}, u32[]{:S(2)}) collective-permute-start(f32[32,128]{1,0:T(8,128)S(1)} %total.1), channel_id=1, source_target_pairs={{0,16},{1,17},{2,18},{3,19},{4,20},{5,21},{6,22},{7,23},{8,24},{9,... | collective-permute-start | bytes 49160 | tf_op jit(solution)/shard_map/ppermute | solution.py:210
  30.1 0.0 copy-done
  30.1 0.0 copy-done.2
  30.1 0.7 scores.1
  30.8 0.0 collective-permute-done.2.refs_2_
  30.8 0.0 collective-permute-done.1.refs_1_
  30.8 0.7 collective-permute-done.refs_0_
  31.5 0.0 copy-start.1
  31.5 10.8 %all_to_all.21 = f32[16,32,128]{2,1,0:T(8,128)S(1)} all-to-all(f32[16,32,128]{2,1,0:T(8,128)S(1)} %earlier.1), channel_id=1, replica_groups={{0,1,2,3,4,5,6,7,8,9,10,11,12,13,14,15},{16,17,18,19,20,21,22,23,24,25,..., dimensions={0} | all-to-all | bytes 524288 | tf_op jit(solution)/shard_map/all_to_all | solution.py:206
  42.3 0.0 copy-done.1
  42.3 1.6 %attn.1 = (bf16[128,1024]{1,0:T(8,128)(2,1)}, bf16[128,1024]{1,0:T(8,128)(2,1)S(1)}, f32[64,16,128]{2,1,0:T(8,128)}) custom-call(f32[8,64,128]{2,1,0:T(8,128)S(1)} %bitcast.16, bf16[128,1024]{1,0:T(8,128)(2,1)S(1)} %bitcast.14, f32[128,1024]{1,0:T(8,128)S(1)} %get-tuple-element.38.intra_ref, f32[1,1024]{1,0:T(1,128)S(1)} %get-tuple-element.39.gain_ref, ...), custom_call_target="tpu_custom_call" | custom-call | flops 67108864 | bytes 2363392 | tf_op jit(solution)/shard_map/attn/pallas_call | solution.py:189
  43.9 8.8 %all-to-all-start.2 = ((f32[64,16,128]{2,1,0:T(8,128)}), f32[64,16,128]{2,1,0:T(8,128)S(1)}, u32[]{:S(2)}, u32[]{:S(2)}) async-start(f32[64,16,128]{2,1,0:T(8,128)} %get-tuple-element.43), calls=%async_computation.2 | async-start | bytes 1048576 | tf_op jit(solution)/shard_map/all_to_all | solution.py:206
  52.7 2.2 %local.1 = (bf16[128,1024]{1,0:T(8,128)(2,1)}, f32[128,1024]{1,0:T(8,128)S(1)}, f32[128,1024]{1,0:T(8,128)S(1)}) custom-call(f32[8,64,128]{2,1,0:T(8,128)S(1)} %bitcast.17, bf16[128,1024]{1,0:T(8,128)(2,1)S(1)} %bitcast.15, bf16[128,1024]{1,0:T(8,128)(2,1)S(1)} %get-tuple-element.31.k_ref, bf16[128,1024]{1,0:T(8,128)(2,1)S(1)} %get-tuple-element.32.v_ref, ...), custom_call_target="tpu_custom_call" | custom-call | flops 335544320 | bytes 2621440 | tf_op jit(solution)/shard_map/local/pallas_call | solution.py:189
  54.8 15.4 %all-to-all-done.2.x_ref = f32[64,16,128]{2,1,0:T(8,128)S(1)} async-done(((f32[64,16,128]{2,1,0:T(8,128)}), f32[64,16,128]{2,1,0:T(8,128)S(1)}, u32[]{:S(2)}, u32[]{:S(2)}) %all-to-all-start.2) | async-done | bytes 524320 | tf_op jit(solution)/shard_map/all_to_all | solution.py:206
  70.2 0.8 later_sums.1
  71.0 5.9 %all-to-all-start.3 = ((f32[64,8,128]{2,1,0:T(8,128)}), f32[64,8,128]{2,1,0:T(8,128)S(1)}, u32[]{:S(2)}, u32[]{:S(2)}) async-start(f32[64,8,128]{2,1,0:T(8,128)} %get-tuple-element.47), calls=%async_computation.3 | async-start | bytes 524288 | tf_op jit(solution)/shard_map/all_to_all | solution.py:206
  76.9 18.2 %psum.7 = f32[8,128]{1,0:T(8,128)} all-reduce(f32[8,128]{1,0:T(8,128)S(1)} %get-tuple-element.48), channel_id=1, replica_groups=mesh['dp'=8,'ctx'=64] {'dp'}, use_global_device_ids=true, to_apply=%region_0.0 | all-reduce | flops 1024 | bytes 8192 | tf_op jit(solution)/shard_map/psum | solution.py:273
  95.1 0.0 all-to-all-done.3
  95.1 1.2 %later.1 = (bf16[128,1024]{1,0:T(8,128)(2,1)}, bf16[128,1024]{1,0:T(8,128)(2,1)}) custom-call(f32[8,64,128]{2,1,0:T(8,128)S(1)} %bitcast.18, bf16[128,1024]{1,0:T(8,128)(2,1)S(1)} %get-tuple-element.31.k_ref, bf16[128,1024]{1,0:T(8,128)(2,1)S(1)} %get-tuple-element.32.v_ref, f32[128,1024]{1,0:T(8,128)S(1)} %get-tuple-element.50.gk_ref, ...), custom_call_target="tpu_custom_call" | custom-call | flops 67108864 | bytes 2359296 | tf_op jit(solution)/shard_map/later/pallas_call | solution.py:189
  (3 shorter events, 0.0 us)
Async XLA Ops:
  16.2 13.8 %copy-start = (bf16[1,128,1024]{2,1,0:T(8,128)(2,1)S(1)}, bf16[1,128,1024]{2,1,0:T(8,128)(2,1)}, u32[]{:S(2)}) copy-start(bf16[1,128,1024]{2,1,0:T(8,128)(2,1)} %param.5) | copy-start | bytes 786436
  16.3 13.8 %copy-start.2 = (f32[1024]{0:T(1024)S(1)}, f32[1024]{0:T(1024)}, u32[]{:S(2)}) copy-start(f32[1024]{0:T(1024)} %param.8) | copy-start | bytes 12292
  16.3 14.5 %collective-permute-start.2 = (f32[32,128]{1,0:T(8,128)S(1)}, f32[32,128]{1,0:T(8,128)S(1)}, u32[]{:S(2)}, u32[]{:S(2)}) collective-permute-start(f32[32,128]{1,0:T(8,128)S(1)} %total.1), channel_id=1, source_target_pairs={{0,48},{1,49},{2,50},{3,51},{4,52},{5,53},{6,54},{7,55},{8,56},{9,... | collective-permute-start | bytes 49160 | tf_op jit(solution)/shard_map/ppermute | solution.py:210
  24.5 6.3 %collective-permute-start.1 = (f32[32,128]{1,0:T(8,128)S(1)}, f32[32,128]{1,0:T(8,128)S(1)}, u32[]{:S(2)}, u32[]{:S(2)}) collective-permute-start(f32[32,128]{1,0:T(8,128)S(1)} %total.1), channel_id=1, source_target_pairs={{0,32},{1,33},{2,34},{3,35},{4,36},{5,37},{6,38},{7,39},{8,40},{9,... | collective-permute-start | bytes 49160 | tf_op jit(solution)/shard_map/ppermute | solution.py:210
  25.8 5.7 %collective-permute-start = (f32[32,128]{1,0:T(8,128)S(1)}, f32[32,128]{1,0:T(8,128)S(1)}, u32[]{:S(2)}, u32[]{:S(2)}) collective-permute-start(f32[32,128]{1,0:T(8,128)S(1)} %total.1), channel_id=1, source_target_pairs={{0,16},{1,17},{2,18},{3,19},{4,20},{5,21},{6,22},{7,23},{8,24},{9,... | collective-permute-start | bytes 49160 | tf_op jit(solution)/shard_map/ppermute | solution.py:210
  31.5 10.8 %copy-start.1 = (bf16[1,128,1024]{2,1,0:T(8,128)(2,1)S(1)}, bf16[1,128,1024]{2,1,0:T(8,128)(2,1)}, u32[]{:S(2)}) copy-start(bf16[1,128,1024]{2,1,0:T(8,128)(2,1)} %param.9) | copy-start | bytes 786436
  43.9 26.3 %all-to-all-start.2 = ((f32[64,16,128]{2,1,0:T(8,128)}), f32[64,16,128]{2,1,0:T(8,128)S(1)}, u32[]{:S(2)}, u32[]{:S(2)}) async-start(f32[64,16,128]{2,1,0:T(8,128)} %get-tuple-element.43), calls=%async_computation.2 | async-start | bytes 1048576 | tf_op jit(solution)/shard_map/all_to_all | solution.py:206
  71.0 24.1 %all-to-all-start.3 = ((f32[64,8,128]{2,1,0:T(8,128)}), f32[64,8,128]{2,1,0:T(8,128)S(1)}, u32[]{:S(2)}, u32[]{:S(2)}) async-start(f32[64,8,128]{2,1,0:T(8,128)} %get-tuple-element.47), calls=%async_computation.3 | async-start | bytes 524288 | tf_op jit(solution)/shard_map/all_to_all | solution.py:206

commit v3 on v2

--- a/solution.py
+++ b/solution.py
@@ -84,11 +84,9 @@
     gain_out[...] = gain_ref[...]
 
 
-def attn_kernel(state_ref, q_ref, intra_ref, gain_ref, g_ref, out_ref, ga_ref, sent_ref, attn_ref, gg_ref):
+def attn_kernel(state_ref, q_ref, intra_ref, gain_ref, g_ref, out_ref, ga_ref, sums_ref, attn_ref):
     rows, width = q_ref.shape
     pairs = width // PAIR
-    part = sent_ref.shape[1] - pairs
-    per = HEAD_DIM // part
     masks = halves()
     square = jnp.zeros((rows, PAIR), F32)
     for p in range(pairs):
@@ -104,17 +102,15 @@
         gain = gain_ref[:, cols(p)]
         out_ref[:, cols(p)] = (normed * gain).astype(BF16)
         gn = g_ref[:, cols(p)].astype(F32) * normed
-        gg_ref[p : p + 1, :] = jnp.sum(gn, 0, keepdims=True)
+        row = pairs * HEAD_DIM + p
+        sums_ref[row : row + 1, :] = jnp.sum(gn, 0, keepdims=True)
         dots = dots + gn * gain
     mean = jnp.sum(dots, 1, keepdims=True) * (1.0 / width)
     for p in range(pairs):
         dn = g_ref[:, cols(p)].astype(F32) * gain_ref[:, cols(p)]
         ga = (inv * (dn - attn_ref[:, cols(p)] * mean)).astype(BF16)
         ga_ref[:, cols(p)] = ga
-        sent_ref[per * p : per * (p + 1), :part, :] = pack(mm_at(q_ref[:, cols(p)], ga)).reshape(per, part, PAIR)
-    own = gg_ref[...]
-    for i in range(sent_ref.shape[0]):
-        sent_ref[i, part:, :] = own
+        sums_ref[p * HEAD_DIM : (p + 1) * HEAD_DIM, :] = pack(mm_at(q_ref[:, cols(p)], ga))
 
 
 def local_kernel(state_ref, q_ref, k_ref, v_ref, ga_ref, gq_ref, gk_ref, gv_ref):
@@ -144,10 +140,32 @@
         gv_ref[:, cols(p)] = mm(sct, ga2)
 
 
-def later_kernel(later_ref, k_ref, v_ref, gk_ref, gv_ref, gk_out, gv_out):
+def first_core():
+    return lax.rem(lax.axis_index("ctx"), 2) == 0
+
+
+def merge_kernel(gains, mine_ref, got_ref, o_ref):
+    first = first_core()
+    chips = o_ref.shape[0]
+    part = o_ref.shape[1] - gains
+    rows = chips * part
+    gain = mine_ref[2 * rows :, :] + got_ref[2 * rows :, :]
+    for i in range(chips):
+        low, high = slice(i * part, (i + 1) * part), slice(rows + i * part, rows + (i + 1) * part)
+        o_ref[i, :part, :] = jnp.where(first, mine_ref[low, :] + got_ref[low, :], mine_ref[high, :] + got_ref[high, :])
+        o_ref[i, part:, :] = gain
+
+
+def later_kernel(sums_ref, got_ref, k_ref, v_ref, gk_ref, gv_ref, gk_out, gv_out):
+    first = first_core()
     masks = halves()
-    for p in range(k_ref.shape[1] // PAIR):
-        low = stack(later_ref[p].astype(BF16), masks)
+    pairs = k_ref.shape[1] // PAIR
+    for p in range(pairs):
+        core, i = divmod(p, pairs // 2)
+        per = sums_ref.shape[0] // (pairs // 2)
+        later = sums_ref[per * i : per * (i + 1), core].reshape(HEAD_DIM, PAIR)
+        later = later + jnp.where(first, got_ref[p * HEAD_DIM : (p + 1) * HEAD_DIM, :], 0.0)
+        low = stack(later.astype(BF16), masks)
         gk_out[:, cols(p)] = (gk_ref[:, cols(p)] + mm_bt(v_ref[:, cols(p)], low)).astype(BF16)
         gv_out[:, cols(p)] = (gv_ref[:, cols(p)] + mm(k_ref[:, cols(p)], low)).astype(BF16)
 
@@ -174,7 +192,8 @@
     acc = jnp.zeros((part, PAIR), F32)
     gain = jnp.zeros(gg_ref.shape, F32)
     for i in reversed(range(x_ref.shape[0])):
-        o_ref[i] = acc
+        o_ref[2 * i] = acc
+        o_ref[2 * i + 1] = acc
         acc = acc + x_ref[i, :part, :]
         gain = gain + x_ref[i, part:, :]
     gg_ref[...] = gain
@@ -200,6 +219,9 @@
 
 def make(ctx, members):
     groups = ctx // members
+    chips = ctx // 2
+    same_core = [[2 * m + c for m in range(chips)] for c in range(2)]
+    neighbour = [(i, i ^ 1) for i in range(ctx)]
     inside = [[g * members + r for r in range(members)] for g in range(groups)]
 
     def exchange(x, devices=None):
@@ -242,16 +264,25 @@
         sent, intra, *outside = lax.optimization_barrier((sent, intra, *outside))
         before = call(earlier_kernel, (sds(piece, F32),), (sent, *outside), "earlier", 0)
         state = exchange(before, inside).reshape(state_shape)
-        out, ga, sent = call(
+        out, ga, mine = call(
             attn_kernel,
-            (sds((rows, width), BF16), sds((rows, width), BF16), sds((ctx, small + pairs, PAIR), F32)),
+            (tile, tile, sds((pairs * HEAD_DIM + pairs, PAIR), F32)),
             (state, q, intra, gain, g),
             "attn",
             2 * flops,
-            scratch=(pltpu.VMEM((rows, width), F32), pltpu.VMEM((pairs, PAIR), F32)),
-            near=(False, True, False),
-        )
-        sent = exchange(sent)
+            scratch=(pltpu.VMEM((rows, width), F32),),
+            near=(False, True, True),
+        )
+        got = lax.ppermute(mine, "ctx", neighbour)
+        sent = call(
+            functools.partial(merge_kernel, pairs),
+            (sds((chips, small + pairs, PAIR), F32),),
+            (mine, got),
+            "merge",
+            0,
+            near=(False,),
+        )
+        sent = exchange(sent, same_core)
         gq, gk, gv = call(
             local_kernel,
             (sds((rows, width), BF16), sds((rows, width), F32), sds((rows, width), F32)),
@@ -269,13 +300,13 @@
             0,
             near=(False, True),
         )
-        later = exchange(after).reshape(state_shape)
+        later = exchange(after)
         gg = lax.psum(gg, "dp")
         later, gg = lax.optimization_barrier((later, gg))
         gk, gv = call(
             later_kernel,
-            (sds((rows, width), BF16), sds((rows, width), BF16)),
-            (later, k, v, gk, gv),
+            (tile, tile),
+            (later.reshape(chips, 2, small, PAIR), got, k, v, gk, gv),
             "later",
             2 * flops,
             near=(False, False),

time: 96.7 us -> 94.6 us (0.978)
  waiting for transfers between devices: 16.1 us -> 11.4 us
  starting transfers between devices: 28.4 us -> 30.5 us
    all_to_all x2, waiting for transfers between devices: 15.4 us -> 9.51 us  [exchange(): return lax.all_to_all(x, 'ctx', 0, 0, tiled=True, axis_index_groups=devices)]
    ppermute x0 -> x1, starting transfers between devices: none -> 2.66 us  [per_device(): got = lax.ppermute(mine, 'ctx', neighbour)]
    ppermute x0 -> x1, waiting for transfers between devices: none -> 1.15 us  [per_device(): got = lax.ppermute(mine, 'ctx', neighbour)]
    pallas_call x8 -> x9, Pallas kernels: 8.13 us -> 8.6 us  [call(): pl.pallas_call(kernel, out_shape=shapes[0] if single else shapes, in_spec...]
  transfers between devices with their start and end apart: 5 -> 6, of which waited for: 2 -> 3; matrix products, arithmetic and copies ran while one was open for 0% -> 0% of each run, Pallas kernels for 3% -> 3%
where the time goes in v3:
time: 94.6 us; the launch traced here: 94.1 us
  blocking collectives  42.8 us (45%)
  starting transfers between devices  30.5 us (32%)
  waiting for transfers between devices  11.4 us (12%)
  Pallas kernels  8.6 us (9%)
    all_to_all x2, blocking collectives, exchange(): return lax.all_to_all(x, 'ctx', 0, 0, tiled=True, axis_index_groups=devices)  24.6 us
    psum x1, blocking collectives, per_device(): gg = lax.psum(gg, 'dp')  18.2 us
    all_to_all x2, starting transfers between devices, exchange(): return lax.all_to_all(x, 'ctx', 0, 0, tiled=True, axis_index_groups=devices)  14.1 us
    ppermute x3, starting transfers between devices, from_earlier(): lax.ppermute(total, 'ctx', [(i, i + d * members) for i in range(ctx - d *...  13.8 us
    all_to_all x2, waiting for transfers between devices, exchange(): return lax.all_to_all(x, 'ctx', 0, 0, tiled=True, axis_index_groups=devices)  9.51 us
    pallas_call x9, Pallas kernels, call(): pl.pallas_call(kernel, out_shape=shapes[0] if single else shapes, in_spec...  8.6 us
    ppermute x1, starting transfers between devices, per_device(): got = lax.ppermute(mine, 'ctx', neighbour)  2.66 us
  transfers between devices with their start and end apart: 6, of which 3 were waited for; matrix products, arithmetic and copies ran while one was open for 0% of the time, Pallas kernels for 3%

profile of v3, /device:TPU:2, one launch (start us, length us, event | category | flops | bytes accessed | tf_op | source)
XLA Modules:
  0.0 94.1 jit_solution(5698795044785842666)
XLA Ops:
  0.6 1.7 %kv.1 = (f32[8,64,128]{2,1,0:T(8,128)S(1)}, bf16[128,1024]{1,0:T(8,128)(2,1)S(1)}, bf16[128,1024]{1,0:T(8,128)(2,1)S(1)}) custom-call(bf16[128,1024]{1,0:T(8,128)(2,1)} %bitcast.22, bf16[128,1024]{1,0:T(8,128)(2,1)} %bitcast.23), custom_call_target="tpu_custom_call" | custom-call | flops 33554432 | bytes 1310720 | tf_op jit(solution)/shard_map/kv/pallas_call | solution.py:208
  2.4 13.9 %all_to_all.20.x_ref = f32[16,32,128]{2,1,0:T(8,128)S(1)} all-to-all(f32[16,32,128]{2,1,0:T(8,128)S(1)} %bitcast.20), channel_id=1, replica_groups={{0,1,2,3,4,5,6,7,8,9,10,11,12,13,14,15},{16,17,18,19,20,21,22,23,24,25,..., dimensions={0} | all-to-all | bytes 524288 | tf_op jit(solution)/shard_map/all_to_all | solution.py:228
  16.3 0.0 copy-start.2
  16.3 8.2 %collective-permute-start.2 = (f32[32,128]{1,0:T(8,128)S(1)}, f32[32,128]{1,0:T(8,128)S(1)}, u32[]{:S(2)}, u32[]{:S(2)}) collective-permute-start(f32[32,128]{1,0:T(8,128)S(1)} %total.1), channel_id=1, source_target_pairs={{0,48},{1,49},{2,50},{3,51},{4,52},{5,53},{6,54},{7,55},{8,56},{9,... | collective-permute-start | bytes 49160 | tf_op jit(solution)/shard_map/ppermute | solution.py:232
  24.5 1.3 %collective-permute-start.1 = (f32[32,128]{1,0:T(8,128)S(1)}, f32[32,128]{1,0:T(8,128)S(1)}, u32[]{:S(2)}, u32[]{:S(2)}) collective-permute-start(f32[32,128]{1,0:T(8,128)S(1)} %total.1), channel_id=1, source_target_pairs={{0,32},{1,33},{2,34},{3,35},{4,36},{5,37},{6,38},{7,39},{8,40},{9,... | collective-permute-start | bytes 49160 | tf_op jit(solution)/shard_map/ppermute | solution.py:232
  25.8 4.3 %collective-permute-start = (f32[32,128]{1,0:T(8,128)S(1)}, f32[32,128]{1,0:T(8,128)S(1)}, u32[]{:S(2)}, u32[]{:S(2)}) collective-permute-start(f32[32,128]{1,0:T(8,128)S(1)} %total.1), channel_id=1, source_target_pairs={{0,16},{1,17},{2,18},{3,19},{4,20},{5,21},{6,22},{7,23},{8,24},{9,... | collective-permute-start | bytes 49160 | tf_op jit(solution)/shard_map/ppermute | solution.py:232
  30.1 0.7 scores.1
  30.8 0.0 collective-permute-done.2.refs_2_
  30.8 0.0 collective-permute-done.1.refs_1_
  30.8 0.7 collective-permute-done.refs_0_
  31.5 0.0 copy-start.1
  31.5 10.8 %all_to_all.21 = f32[16,32,128]{2,1,0:T(8,128)S(1)} all-to-all(f32[16,32,128]{2,1,0:T(8,128)S(1)} %earlier.1), channel_id=1, replica_groups={{0,1,2,3,4,5,6,7,8,9,10,11,12,13,14,15},{16,17,18,19,20,21,22,23,24,25,..., dimensions={0} | all-to-all | bytes 524288 | tf_op jit(solution)/shard_map/all_to_all | solution.py:228
  42.3 1.3 %attn.1 = (bf16[128,1024]{1,0:T(8,128)(2,1)}, bf16[128,1024]{1,0:T(8,128)(2,1)S(1)}, f32[520,128]{1,0:T(8,128)S(1)}) custom-call(f32[8,64,128]{2,1,0:T(8,128)S(1)} %bitcast.16, bf16[128,1024]{1,0:T(8,128)(2,1)S(1)} %bitcast.14, f32[128,1024]{1,0:T(8,128)S(1)} %get-tuple-element.38.intra_ref, f32[1,1024]{1,0:T(1,128)S(1)} %get-tuple-element.39.gain_ref, ...), custom_call_target="tpu_custom_call" | custom-call | flops 67108864 | bytes 2105344 | tf_op jit(solution)/shard_map/attn/pallas_call | solution.py:208
  43.6 2.7 %collective-permute-start.3 = (f32[520,128]{1,0:T(8,128)S(1)}, f32[520,128]{1,0:T(8,128)S(1)}, u32[]{:S(2)}, u32[]{:S(2)}) collective-permute-start(f32[520,128]{1,0:T(8,128)S(1)} %get-tuple-element.43.mine_ref), channel_id=1, source_target_pairs={{0,1},{1,0},{2,3},{3,2},{4,5},{5,4},{6,7},{7,6},{8,9},{9,8},{10,11... | collective-permute-start | bytes 798728 | tf_op jit(solution)/shard_map/ppermute | solution.py:276
  46.3 1.1 %collective-permute-done.3.got_ref = f32[520,128]{1,0:T(8,128)S(1)} collective-permute-done((f32[520,128]{1,0:T(8,128)S(1)}, f32[520,128]{1,0:T(8,128)S(1)}, u32[]{:S(2)}, u32[]{:S(2)}) %collective-permute-start.3) | collective-permute-done | bytes 266272 | tf_op jit(solution)/shard_map/ppermute | solution.py:276
  47.5 0.7 merge.1
  48.2 8.0 %all-to-all-start.2 = ((f32[32,16,128]{2,1,0:T(8,128)}), f32[32,16,128]{2,1,0:T(8,128)S(1)}, u32[]{:S(2)}, u32[]{:S(2)}) async-start(f32[32,16,128]{2,1,0:T(8,128)} %merge.1), calls=%async_computation.2 | async-start | bytes 524288 | tf_op jit(solution)/shard_map/all_to_all | solution.py:228
  56.2 2.2 %local.1 = (bf16[128,1024]{1,0:T(8,128)(2,1)}, f32[128,1024]{1,0:T(8,128)S(1)}, f32[128,1024]{1,0:T(8,128)S(1)}) custom-call(f32[8,64,128]{2,1,0:T(8,128)S(1)} %bitcast.17, bf16[128,1024]{1,0:T(8,128)(2,1)S(1)} %bitcast.15, bf16[128,1024]{1,0:T(8,128)(2,1)S(1)} %get-tuple-element.31.k_ref, bf16[128,1024]{1,0:T(8,128)(2,1)S(1)} %get-tuple-element.32.v_ref, ...), custom_call_target="tpu_custom_call" | custom-call | flops 335544320 | bytes 2621440 | tf_op jit(solution)/shard_map/local/pallas_call | solution.py:208
  58.4 9.5 %all-to-all-done.2.x_ref = f32[32,16,128]{2,1,0:T(8,128)S(1)} async-done(((f32[32,16,128]{2,1,0:T(8,128)}), f32[32,16,128]{2,1,0:T(8,128)S(1)}, u32[]{:S(2)}, u32[]{:S(2)}) %all-to-all-start.2) | async-done | bytes 262176 | tf_op jit(solution)/shard_map/all_to_all | solution.py:228
  67.9 0.7 later_sums.1
  68.6 6.1 %all-to-all-start.3 = ((f32[64,8,128]{2,1,0:T(8,128)}), f32[64,8,128]{2,1,0:T(8,128)S(1)}, u32[]{:S(2)}, u32[]{:S(2)}) async-start(f32[64,8,128]{2,1,0:T(8,128)} %get-tuple-element.47), calls=%async_computation.3 | async-start | bytes 524288 | tf_op jit(solution)/shard_map/all_to_all | solution.py:228
  74.7 18.2 %psum.7 = f32[8,128]{1,0:T(8,128)} all-reduce(f32[8,128]{1,0:T(8,128)S(1)} %get-tuple-element.48), channel_id=1, replica_groups=mesh['dp'=8,'ctx'=64] {'dp'}, use_global_device_ids=true, to_apply=%region_0.0 | all-reduce | flops 1024 | bytes 8192 | tf_op jit(solution)/shard_map/psum | solution.py:304
  92.9 0.0 all-to-all-done.3
  92.9 1.2 %later.1 = (bf16[128,1024]{1,0:T(8,128)(2,1)}, bf16[128,1024]{1,0:T(8,128)(2,1)}) custom-call(f32[32,2,8,128]{3,2,1,0:T(8,128)S(1)} %bitcast.18, f32[520,128]{1,0:T(8,128)S(1)} %collective-permute-done.3.got_ref, bf16[128,1024]{1,0:T(8,128)(2,1)S(1)} %get-tuple-element.31.k_ref, bf16[128,1024]{1,0:T(8,128)(2,1)S(1)} %get-tuple-element.32.v_ref, ...), custom_call_target="tpu_custom_call" | custom-call | flops 67108864 | bytes 2625536 | tf_op jit(solution)/shard_map/later/pallas_call | solution.py:208
  (6 shorter events, 0.0 us)
Async XLA Ops:
  16.2 13.8 %copy-start = (bf16[1,128,1024]{2,1,0:T(8,128)(2,1)S(1)}, bf16[1,128,1024]{2,1,0:T(8,128)(2,1)}, u32[]{:S(2)}) copy-start(bf16[1,128,1024]{2,1,0:T(8,128)(2,1)} %param.5) | copy-start | bytes 786436
  16.3 13.8 %copy-start.2 = (f32[1024]{0:T(1024)S(1)}, f32[1024]{0:T(1024)}, u32[]{:S(2)}) copy-start(f32[1024]{0:T(1024)} %param.8) | copy-start | bytes 12292
  16.3 14.5 %collective-permute-start.2 = (f32[32,128]{1,0:T(8,128)S(1)}, f32[32,128]{1,0:T(8,128)S(1)}, u32[]{:S(2)}, u32[]{:S(2)}) collective-permute-start(f32[32,128]{1,0:T(8,128)S(1)} %total.1), channel_id=1, source_target_pairs={{0,48},{1,49},{2,50},{3,51},{4,52},{5,53},{6,54},{7,55},{8,56},{9,... | collective-permute-start | bytes 49160 | tf_op jit(solution)/shard_map/ppermute | solution.py:232
  24.5 6.3 %collective-permute-start.1 = (f32[32,128]{1,0:T(8,128)S(1)}, f32[32,128]{1,0:T(8,128)S(1)}, u32[]{:S(2)}, u32[]{:S(2)}) collective-permute-start(f32[32,128]{1,0:T(8,128)S(1)} %total.1), channel_id=1, source_target_pairs={{0,32},{1,33},{2,34},{3,35},{4,36},{5,37},{6,38},{7,39},{8,40},{9,... | collective-permute-start | bytes 49160 | tf_op jit(solution)/shard_map/ppermute | solution.py:232
  25.8 5.7 %collective-permute-start = (f32[32,128]{1,0:T(8,128)S(1)}, f32[32,128]{1,0:T(8,128)S(1)}, u32[]{:S(2)}, u32[]{:S(2)}) collective-permute-start(f32[32,128]{1,0:T(8,128)S(1)} %total.1), channel_id=1, source_target_pairs={{0,16},{1,17},{2,18},{3,19},{4,20},{5,21},{6,22},{7,23},{8,24},{9,... | collective-permute-start | bytes 49160 | tf_op jit(solution)/shard_map/ppermute | solution.py:232
  31.5 10.8 %copy-start.1 = (bf16[1,128,1024]{2,1,0:T(8,128)(2,1)S(1)}, bf16[1,128,1024]{2,1,0:T(8,128)(2,1)}, u32[]{:S(2)}) copy-start(bf16[1,128,1024]{2,1,0:T(8,128)(2,1)} %param.9) | copy-start | bytes 786436
  43.6 3.8 %collective-permute-start.3 = (f32[520,128]{1,0:T(8,128)S(1)}, f32[520,128]{1,0:T(8,128)S(1)}, u32[]{:S(2)}, u32[]{:S(2)}) collective-permute-start(f32[520,128]{1,0:T(8,128)S(1)} %get-tuple-element.43.mine_ref), channel_id=1, source_target_pairs={{0,1},{1,0},{2,3},{3,2},{4,5},{5,4},{6,7},{7,6},{8,9},{9,8},{10,11... | collective-permute-start | bytes 798728 | tf_op jit(solution)/shard_map/ppermute | solution.py:276
  48.2 19.7 %all-to-all-start.2 = ((f32[32,16,128]{2,1,0:T(8,128)}), f32[32,16,128]{2,1,0:T(8,128)S(1)}, u32[]{:S(2)}, u32[]{:S(2)}) async-start(f32[32,16,128]{2,1,0:T(8,128)} %merge.1), calls=%async_computation.2 | async-start | bytes 524288 | tf_op jit(solution)/shard_map/all_to_all | solution.py:228
  68.6 24.3 %all-to-all-start.3 = ((f32[64,8,128]{2,1,0:T(8,128)}), f32[64,8,128]{2,1,0:T(8,128)S(1)}, u32[]{:S(2)}, u32[]{:S(2)}) async-start(f32[64,8,128]{2,1,0:T(8,128)} %get-tuple-element.47), calls=%async_computation.3 | async-start | bytes 524288 | tf_op jit(solution)/shard_map/all_to_all | solution.py:228

commit v4 on v3

--- a/solution.py
+++ b/solution.py
@@ -84,7 +84,7 @@
     gain_out[...] = gain_ref[...]
 
 
-def attn_kernel(state_ref, q_ref, intra_ref, gain_ref, g_ref, out_ref, ga_ref, sums_ref, attn_ref):
+def attn_kernel(state_ref, q_ref, intra_ref, gain_ref, g_ref, attn_ref, ga_ref, sums_ref):
     rows, width = q_ref.shape
     pairs = width // PAIR
     masks = halves()
@@ -100,7 +100,6 @@
         normed = attn_ref[:, cols(p)] * inv
         attn_ref[:, cols(p)] = normed
         gain = gain_ref[:, cols(p)]
-        out_ref[:, cols(p)] = (normed * gain).astype(BF16)
         gn = g_ref[:, cols(p)].astype(F32) * normed
         row = pairs * HEAD_DIM + p
         sums_ref[row : row + 1, :] = jnp.sum(gn, 0, keepdims=True)
@@ -113,7 +112,7 @@
         sums_ref[p * HEAD_DIM : (p + 1) * HEAD_DIM, :] = pack(mm_at(q_ref[:, cols(p)], ga))
 
 
-def local_kernel(state_ref, q_ref, k_ref, v_ref, ga_ref, gq_ref, gk_ref, gv_ref):
+def local_kernel(state_ref, q_ref, k_ref, v_ref, ga_ref, normed_ref, gain_ref, out_ref, gq_ref, gk_ref, gv_ref):
     rows = q_ref.shape[0]
     masks = halves()
     t = lax.broadcasted_iota(jnp.int32, (rows, rows), 0)
@@ -126,6 +125,7 @@
 
     for p in range(q_ref.shape[1] // PAIR):
         q, k, v, ga = q_ref[:, cols(p)], k_ref[:, cols(p)], v_ref[:, cols(p)], ga_ref[:, cols(p)]
+        out_ref[:, cols(p)] = (normed_ref[:, cols(p)] * gain_ref[:, cols(p)]).astype(BF16)
         low = state_ref[p].astype(BF16)
         ga2, q2 = stack(ga, masks), stack(q, masks)
         ds = mm_bt(ga2, v)
@@ -174,15 +174,17 @@
     total = x_ref[0]
     for i in range(1, x_ref.shape[0]):
         total = total + x_ref[i]
-    o_ref[...] = total
-
-
-def earlier_kernel(x_ref, *refs):
-    outside, o_ref = refs[:-1], refs[-1]
+    for i in range(o_ref.shape[0]):
+        o_ref[i] = total
+
+
+def earlier_kernel(x_ref, z_ref, o_ref):
+    members = x_ref.shape[0]
+    group = lax.div(lax.axis_index("ctx"), members)
     acc = jnp.zeros(o_ref.shape[1:], F32)
-    for ref in outside:
-        acc = acc + ref[...]
-    for i in range(x_ref.shape[0]):
+    for i in range(z_ref.shape[0] - 1):
+        acc = acc + jnp.where(group > i, z_ref[i], 0.0)
+    for i in range(members):
         o_ref[i] = acc
         acc = acc + x_ref[i]
 
@@ -222,16 +224,11 @@
     chips = ctx // 2
     same_core = [[2 * m + c for m in range(chips)] for c in range(2)]
     neighbour = [(i, i ^ 1) for i in range(ctx)]
+    across = [[g * members + r for g in range(groups)] for r in range(members)]
     inside = [[g * members + r for r in range(members)] for g in range(groups)]
 
     def exchange(x, devices=None):
         return lax.all_to_all(x, "ctx", 0, 0, tiled=True, axis_index_groups=devices)
-
-    def from_earlier(total):
-        return [
-            lax.ppermute(total, "ctx", [(i, i + d * members) for i in range(ctx - d * members)])
-            for d in range(1, groups)
-        ]
 
     def per_device(queries, keys, values, gain, grad_out):
         _, rows, width = queries.shape
@@ -256,22 +253,19 @@
             far=True,
         )
         sent = exchange(kv.reshape(piece), inside)
-        total = call(total_kernel, (sds((part, PAIR), F32),), (sent,), "total", 0)
-        outside = from_earlier(total)
+        totals = call(total_kernel, (sds((groups, part, PAIR), F32),), (sent,), "totals", 0)
+        totals = exchange(totals, across)
         intra, gain = call(
             scores_kernel, (sds((rows, width), F32), sds((1, width), F32)), (q, k, v, gain), "scores", 4 * flops
         )
-        sent, intra, *outside = lax.optimization_barrier((sent, intra, *outside))
-        before = call(earlier_kernel, (sds(piece, F32),), (sent, *outside), "earlier", 0)
+        before = call(earlier_kernel, (sds(piece, F32),), (sent, totals), "earlier", 0)
         state = exchange(before, inside).reshape(state_shape)
-        out, ga, mine = call(
+        normed, ga, mine = call(
             attn_kernel,
-            (tile, tile, sds((pairs * HEAD_DIM + pairs, PAIR), F32)),
+            (sds((rows, width), F32), tile, sds((pairs * HEAD_DIM + pairs, PAIR), F32)),
             (state, q, intra, gain, g),
             "attn",
             2 * flops,
-            scratch=(pltpu.VMEM((rows, width), F32),),
-            near=(False, True, True),
         )
         got = lax.ppermute(mine, "ctx", neighbour)
         sent = call(
@@ -283,13 +277,13 @@
             near=(False,),
         )
         sent = exchange(sent, same_core)
-        gq, gk, gv = call(
+        out, gq, gk, gv = call(
             local_kernel,
-            (sds((rows, width), BF16), sds((rows, width), F32), sds((rows, width), F32)),
-            (state, q, k, v, ga),
+            (tile, tile, sds((rows, width), F32), sds((rows, width), F32)),
+            (state, q, k, v, ga, normed, gain),
             "local",
             10 * flops,
-            near=(False, True, True),
+            near=(False, False, True, True),
         )
         sent, gk, gv = lax.optimization_barrier((sent, gk, gv))
         after, gg = call(

time: 94.6 us -> 93.9 us (level)
  starting transfers between devices: 30.5 us -> 20.4 us
  blocking collectives: 42.8 us -> 47.9 us
  waiting for transfers between devices: 11.4 us -> 14.9 us
    ppermute x3 -> x0, starting transfers between devices: 13.8 us -> none  [from_earlier(): lax.ppermute(total, 'ctx', [(i, i + d * members) for i in range(ctx - d *...]
    all_to_all x2, blocking collectives: 24.6 us -> 29.6 us  [exchange(): return lax.all_to_all(x, 'ctx', 0, 0, tiled=True, axis_index_groups=devices)]
    all_to_all x2 -> x3, waiting for transfers between devices: 9.51 us -> 13.7 us  [exchange(): return lax.all_to_all(x, 'ctx', 0, 0, tiled=True, axis_index_groups=devices)]
    all_to_all x2 -> x3, starting transfers between devices: 14.1 us -> 17.7 us  [exchange(): return lax.all_to_all(x, 'ctx', 0, 0, tiled=True, axis_index_groups=devices)]
  transfers between devices with their start and end apart: 6 -> 4, of which waited for: 3 -> 3; matrix products, arithmetic and copies ran while one was open for 0% -> 0% of each run, Pallas kernels for 3% -> 3%
where the time goes in v4:
time: 93.9 us; the launch traced here: 93.3 us
  blocking collectives  47.9 us (51%)
  starting transfers between devices  20.4 us (22%)
  waiting for transfers between devices  14.9 us (16%)
  Pallas kernels  8.86 us (9%)
    all_to_all x2, blocking collectives, exchange(): return lax.all_to_all(x, 'ctx', 0, 0, tiled=True, axis_index_groups=devices)  29.6 us
    psum x1, blocking collectives, per_device(): gg = lax.psum(gg, 'dp')  18.2 us
    all_to_all x3, starting transfers between devices, exchange(): return lax.all_to_all(x, 'ctx', 0, 0, tiled=True, axis_index_groups=devices)  17.7 us
    all_to_all x3, waiting for transfers between devices, exchange(): return lax.all_to_all(x, 'ctx', 0, 0, tiled=True, axis_index_groups=devices)  13.7 us
    pallas_call x9, Pallas kernels, call(): pl.pallas_call(kernel, out_shape=shapes[0] if single else shapes, in_spec...  8.86 us
    ppermute x1, starting transfers between devices, per_device(): got = lax.ppermute(mine, 'ctx', neighbour)  2.68 us
  transfers between devices with their start and end apart: 4, of which 3 were waited for; matrix products, arithmetic and copies ran while one was open for 0% of the time, Pallas kernels for 3%

profile of v4, /device:TPU:2, one launch (start us, length us, event | category | flops | bytes accessed | tf_op | source)
XLA Modules:
  0.0 93.3 jit_solution(15062111658255868296)
XLA Ops:
  0.6 1.7 %kv.1 = (f32[8,64,128]{2,1,0:T(8,128)S(1)}, bf16[128,1024]{1,0:T(8,128)(2,1)S(1)}, bf16[128,1024]{1,0:T(8,128)(2,1)S(1)}) custom-call(bf16[128,1024]{1,0:T(8,128)(2,1)} %bitcast.22, bf16[128,1024]{1,0:T(8,128)(2,1)} %bitcast.23), custom_call_target="tpu_custom_call" | custom-call | flops 33554432 | bytes 1310720 | tf_op jit(solution)/shard_map/kv/pallas_call | solution.py:210
  2.4 13.9 %all_to_all.25.x_ref = f32[16,32,128]{2,1,0:T(8,128)S(1)} all-to-all(f32[16,32,128]{2,1,0:T(8,128)S(1)} %bitcast.20), channel_id=1, replica_groups={{0,1,2,3,4,5,6,7,8,9,10,11,12,13,14,15},{16,17,18,19,20,21,22,23,24,25,..., dimensions={0} | all-to-all | bytes 524288 | tf_op jit(solution)/shard_map/all_to_all | solution.py:231
  16.3 15.8 %all_to_all.26.z_ref = f32[4,32,128]{2,1,0:T(8,128)S(1)} all-to-all(f32[4,32,128]{2,1,0:T(8,128)S(1)} %totals.1), channel_id=1, replica_groups={{0,16,32,48},{1,17,33,49},{2,18,34,50},{3,19,35,51},{4,20,36,52},{5,21,..., dimensions={0} | all-to-all | bytes 131072 | tf_op jit(solution)/shard_map/all_to_all | solution.py:231
  32.0 0.7 earlier.1
  32.8 0.0 copy-start
  32.8 5.8 %all-to-all-start.2 = ((f32[16,32,128]{2,1,0:T(8,128)}), f32[16,32,128]{2,1,0:T(8,128)S(1)}, u32[]{:S(2)}, u32[]{:S(2)}) async-start(f32[16,32,128]{2,1,0:T(8,128)} %earlier.1), calls=%async_computation.2 | async-start | bytes 524288 | tf_op jit(solution)/shard_map/all_to_all | solution.py:231
  38.6 0.0 copy-start.2
  38.6 0.0 copy-done
  38.6 0.7 copy-done.2
  39.3 0.7 scores.1
  40.0 4.2 %all-to-all-done.2 = f32[16,32,128]{2,1,0:T(8,128)S(1)} async-done(((f32[16,32,128]{2,1,0:T(8,128)}), f32[16,32,128]{2,1,0:T(8,128)S(1)}, u32[]{:S(2)}, u32[]{:S(2)}) %all-to-all-start.2) | async-done | bytes 262176 | tf_op jit(solution)/shard_map/all_to_all | solution.py:231
  44.1 0.0 copy-done.1
  44.1 0.7 attn.1
  44.9 2.7 %collective-permute-start = (f32[520,128]{1,0:T(8,128)S(1)}, f32[520,128]{1,0:T(8,128)S(1)}, u32[]{:S(2)}, u32[]{:S(2)}) collective-permute-start(f32[520,128]{1,0:T(8,128)S(1)} %get-tuple-element.35.mine_ref), channel_id=1, source_target_pairs={{0,1},{1,0},{2,3},{3,2},{4,5},{5,4},{6,7},{7,6},{8,9},{9,8},{10,11... | collective-permute-start | bytes 798728 | tf_op jit(solution)/shard_map/ppermute | solution.py:270
  47.5 1.1 %collective-permute-done.got_ref = f32[520,128]{1,0:T(8,128)S(1)} collective-permute-done((f32[520,128]{1,0:T(8,128)S(1)}, f32[520,128]{1,0:T(8,128)S(1)}, u32[]{:S(2)}, u32[]{:S(2)}) %collective-permute-start) | collective-permute-done | bytes 266272 | tf_op jit(solution)/shard_map/ppermute | solution.py:270
  48.7 0.7 merge.1
  49.4 5.8 %all-to-all-start.3 = ((f32[32,16,128]{2,1,0:T(8,128)}), f32[32,16,128]{2,1,0:T(8,128)S(1)}, u32[]{:S(2)}, u32[]{:S(2)}) async-start(f32[32,16,128]{2,1,0:T(8,128)} %merge.1), calls=%async_computation.3 | async-start | bytes 524288 | tf_op jit(solution)/shard_map/all_to_all | solution.py:231
  55.3 2.3 %local.1 = (bf16[128,1024]{1,0:T(8,128)(2,1)}, bf16[128,1024]{1,0:T(8,128)(2,1)}, f32[128,1024]{1,0:T(8,128)S(1)}, f32[128,1024]{1,0:T(8,128)S(1)}) custom-call(f32[8,64,128]{2,1,0:T(8,128)S(1)} %bitcast.17, bf16[128,1024]{1,0:T(8,128)(2,1)S(1)} %bitcast.15, bf16[128,1024]{1,0:T(8,128)(2,1)S(1)} %get-tuple-element.27.k_ref, ...), custom_call_target="tpu_custom_call" | custom-call | flops 335544320 | bytes 3411968 | tf_op jit(solution)/shard_map/local/pallas_call | solution.py:210
  57.6 9.6 %all-to-all-done.3.x_ref = f32[32,16,128]{2,1,0:T(8,128)S(1)} async-done(((f32[32,16,128]{2,1,0:T(8,128)}), f32[32,16,128]{2,1,0:T(8,128)S(1)}, u32[]{:S(2)}, u32[]{:S(2)}) %all-to-all-start.3) | async-done | bytes 262176 | tf_op jit(solution)/shard_map/all_to_all | solution.py:231
  67.1 0.7 later_sums.1
  67.9 6.0 %all-to-all-start.4 = ((f32[64,8,128]{2,1,0:T(8,128)}), f32[64,8,128]{2,1,0:T(8,128)S(1)}, u32[]{:S(2)}, u32[]{:S(2)}) async-start(f32[64,8,128]{2,1,0:T(8,128)} %get-tuple-element.39), calls=%async_computation.4 | async-start | bytes 524288 | tf_op jit(solution)/shard_map/all_to_all | solution.py:231
  73.9 18.2 %psum.7 = f32[8,128]{1,0:T(8,128)} all-reduce(f32[8,128]{1,0:T(8,128)S(1)} %get-tuple-element.40), channel_id=1, replica_groups=mesh['dp'=8,'ctx'=64] {'dp'}, use_global_device_ids=true, to_apply=%region_0.0 | all-reduce | flops 1024 | bytes 8192 | tf_op jit(solution)/shard_map/psum | solution.py:298
  92.1 0.0 all-to-all-done.4
  92.1 1.2 %later.1 = (bf16[128,1024]{1,0:T(8,128)(2,1)}, bf16[128,1024]{1,0:T(8,128)(2,1)}) custom-call(f32[32,2,8,128]{3,2,1,0:T(8,128)S(1)} %bitcast.18, f32[520,128]{1,0:T(8,128)S(1)} %collective-permute-done.got_ref, bf16[128,1024]{1,0:T(8,128)(2,1)S(1)} %get-tuple-element.27.k_ref, bf16[128,1024]{1,0:T(8,128)(2,1)S(1)} %get-tuple-element.28.v_ref, ...), custom_call_target="tpu_custom_call" | custom-call | flops 67108864 | bytes 2625536 | tf_op jit(solution)/shard_map/later/pallas_call | solution.py:210
  (2 shorter events, 0.0 us)
Async XLA Ops:
  32.8 5.8 %copy-start = (bf16[1,128,1024]{2,1,0:T(8,128)(2,1)S(1)}, bf16[1,128,1024]{2,1,0:T(8,128)(2,1)}, u32[]{:S(2)}) copy-start(bf16[1,128,1024]{2,1,0:T(8,128)(2,1)} %param.5) | copy-start | bytes 786436
  32.8 11.3 %all-to-all-start.2 = ((f32[16,32,128]{2,1,0:T(8,128)}), f32[16,32,128]{2,1,0:T(8,128)S(1)}, u32[]{:S(2)}, u32[]{:S(2)}) async-start(f32[16,32,128]{2,1,0:T(8,128)} %earlier.1), calls=%async_computation.2 | async-start | bytes 524288 | tf_op jit(solution)/shard_map/all_to_all | solution.py:231
  38.6 0.7 copy-start.2
  39.3 4.8 %copy-start.1 = (bf16[1,128,1024]{2,1,0:T(8,128)(2,1)S(1)}, bf16[1,128,1024]{2,1,0:T(8,128)(2,1)}, u32[]{:S(2)}) copy-start(bf16[1,128,1024]{2,1,0:T(8,128)(2,1)} %param.9) | copy-start | bytes 786436
  44.9 3.8 %collective-permute-start = (f32[520,128]{1,0:T(8,128)S(1)}, f32[520,128]{1,0:T(8,128)S(1)}, u32[]{:S(2)}, u32[]{:S(2)}) collective-permute-start(f32[520,128]{1,0:T(8,128)S(1)} %get-tuple-element.35.mine_ref), channel_id=1, source_target_pairs={{0,1},{1,0},{2,3},{3,2},{4,5},{5,4},{6,7},{7,6},{8,9},{9,8},{10,11... | collective-permute-start | bytes 798728 | tf_op jit(solution)/shard_map/ppermute | solution.py:270
  49.4 17.7 %all-to-all-start.3 = ((f32[32,16,128]{2,1,0:T(8,128)}), f32[32,16,128]{2,1,0:T(8,128)S(1)}, u32[]{:S(2)}, u32[]{:S(2)}) async-start(f32[32,16,128]{2,1,0:T(8,128)} %merge.1), calls=%async_computation.3 | async-start | bytes 524288 | tf_op jit(solution)/shard_map/all_to_all | solution.py:231
  67.9 24.3 %all-to-all-start.4 = ((f32[64,8,128]{2,1,0:T(8,128)}), f32[64,8,128]{2,1,0:T(8,128)S(1)}, u32[]{:S(2)}, u32[]{:S(2)}) async-start(f32[64,8,128]{2,1,0:T(8,128)} %get-tuple-element.39), calls=%async_computation.4 | async-start | bytes 524288 | tf_op jit(solution)/shard_map/all_to_all | solution.py:231

commit v5 on v4

--- a/solution.py
+++ b/solution.py
@@ -46,7 +46,7 @@
     return slice(p * PAIR, (p + 1) * PAIR)
 
 
-def kv_kernel(k_hbm, v_hbm, kv_ref, k_ref, v_ref, sems):
+def kv_kernel(k_hbm, v_hbm, gain_hbm, kv_ref, k_ref, v_ref, gain_ref, sems, gain_sem):
     chunks = sems.shape[1]
     wide = k_ref.shape[1] // chunks
 
@@ -60,38 +60,33 @@
     for c in range(chunks):
         for copy in copies(c):
             copy.start()
+    gain_copy = pltpu.make_async_copy(gain_hbm, gain_ref, gain_sem)
+    gain_copy.start()
     for c in range(chunks):
         for copy in copies(c):
             copy.wait()
         for p in range(c * wide // PAIR, (c + 1) * wide // PAIR):
             kv_ref[p] = pack(mm_at(k_ref[:, cols(p)], v_ref[:, cols(p)]))
-
-
-def scores_kernel(q_ref, k_ref, v_ref, gain_ref, intra_ref, gain_out):
-    rows = q_ref.shape[0]
+    gain_copy.wait()
+
+
+def attn_kernel(state_ref, q_ref, k_ref, v_ref, gain_ref, g_ref, attn_ref, ga_ref, sums_ref):
+    rows, width = q_ref.shape
+    pairs = width // PAIR
     masks = halves()
     t = lax.broadcasted_iota(jnp.int32, (rows, rows), 0)
     s = lax.broadcasted_iota(jnp.int32, (rows, rows), 1)
     causal = s <= t
-    for p in range(q_ref.shape[1] // PAIR):
+    square = jnp.zeros((rows, PAIR), F32)
+    for p in range(pairs):
         q, k, v = q_ref[:, cols(p)], k_ref[:, cols(p)], v_ref[:, cols(p)]
         sc = mm_bt(stack(q, masks), k)
         sc = jnp.concatenate(
             [jnp.where(causal, sc[:rows], 0.0).astype(BF16), jnp.where(causal, sc[rows:], 0.0).astype(BF16)],
             axis=1,
         )
-        intra_ref[:, cols(p)] = mm(sc, stack(v, masks))
-    gain_out[...] = gain_ref[...]
-
-
-def attn_kernel(state_ref, q_ref, intra_ref, gain_ref, g_ref, attn_ref, ga_ref, sums_ref):
-    rows, width = q_ref.shape
-    pairs = width // PAIR
-    masks = halves()
-    square = jnp.zeros((rows, PAIR), F32)
-    for p in range(pairs):
         low = state_ref[p].astype(BF16)
-        attn = intra_ref[:, cols(p)] + mm(q_ref[:, cols(p)], stack(low, masks))
+        attn = mm(sc, stack(v, masks)) + mm(q, stack(low, masks))
         attn_ref[:, cols(p)] = attn
         square = square + attn * attn
     inv = lax.rsqrt(jnp.sum(square, 1, keepdims=True) * (1.0 / width) + 1e-06)
@@ -243,40 +238,30 @@
         flops = 2 * rows * rows * width
 
         tile = sds((rows, width), BF16)
-        kv, k, v = call(
+        kv, k, v, gain = call(
             kv_kernel,
-            (sds(state_shape, F32), tile, tile),
-            (k, v),
+            (sds(state_shape, F32), tile, tile, sds((1, width), F32)),
+            (k, v, gain),
             "kv",
             flops,
-            scratch=(pltpu.SemaphoreType.DMA((2, 4)),),
+            scratch=(pltpu.SemaphoreType.DMA((2, 4)), pltpu.SemaphoreType.DMA(())),
             far=True,
         )
         sent = exchange(kv.reshape(piece), inside)
         totals = call(total_kernel, (sds((groups, part, PAIR), F32),), (sent,), "totals", 0)
         totals = exchange(totals, across)
-        intra, gain = call(
-            scores_kernel, (sds((rows, width), F32), sds((1, width), F32)), (q, k, v, gain), "scores", 4 * flops
-        )
+        totals = call(total_kernel, (sds((groups, part, PAIR), F32),), (sent,), "totals", 0)
+        totals = exchange(totals, across)
         before = call(earlier_kernel, (sds(piece, F32),), (sent, totals), "earlier", 0)
         state = exchange(before, inside).reshape(state_shape)
         normed, ga, mine = call(
             attn_kernel,
             (sds((rows, width), F32), tile, sds((pairs * HEAD_DIM + pairs, PAIR), F32)),
-            (state, q, intra, gain, g),
+            (state, q, k, v, gain, g),
             "attn",
-            2 * flops,
+            6 * flops,
         )
         got = lax.ppermute(mine, "ctx", neighbour)
-        sent = call(
-            functools.partial(merge_kernel, pairs),
-            (sds((chips, small + pairs, PAIR), F32),),
-            (mine, got),
-            "merge",
-            0,
-            near=(False,),
-        )
-        sent = exchange(sent, same_core)
         out, gq, gk, gv = call(
             local_kernel,
             (tile, tile, sds((rows, width), F32), sds((rows, width), F32)),
@@ -285,7 +270,15 @@
             10 * flops,
             near=(False, False, True, True),
         )
-        sent, gk, gv = lax.optimization_barrier((sent, gk, gv))
+        got, gk, gv = lax.optimization_barrier((got, gk, gv))
+        sent = call(
+            functools.partial(merge_kernel, pairs),
+            (sds((chips, small + pairs, PAIR), F32),),
+            (mine, got),
+            "merge",
+            0,
+        )
+        sent = exchange(sent, same_core)
         after, gg = call(
             later_sums_kernel,
             (sds((ctx, small, PAIR), F32), sds((pairs, PAIR), F32)),

time: 93.9 us -> 92.5 us (0.985)
  blocking collectives: 47.9 us -> 75.1 us
  waiting for transfers between devices: 14.9 us -> 0.01 us
  starting transfers between devices: 20.4 us -> 8.69 us
  Pallas kernels: 8.86 us -> 7.58 us
    all_to_all x2 -> x4, blocking collectives: 29.6 us -> 56.9 us  [exchange(): return lax.all_to_all(x, 'ctx', 0, 0, tiled=True, axis_index_groups=devices)]
    all_to_all x3 -> x1, waiting for transfers between devices: 13.7 us -> 0.01 us  [exchange(): return lax.all_to_all(x, 'ctx', 0, 0, tiled=True, axis_index_groups=devices)]
    all_to_all x3 -> x1, starting transfers between devices: 17.7 us -> 6.01 us  [exchange(): return lax.all_to_all(x, 'ctx', 0, 0, tiled=True, axis_index_groups=devices)]
    pallas_call x9 -> x8, Pallas kernels: 8.86 us -> 7.58 us  [call(): pl.pallas_call(kernel, out_shape=shapes[0] if single else shapes, in_spec...]
    ppermute x1, waiting for transfers between devices: 1.15 us -> 0.01 us  [per_device(): got = lax.ppermute(mine, 'ctx', neighbour)]
  transfers between devices with their start and end apart: 4 -> 2, of which waited for: 3 -> 0; matrix products, arithmetic and copies ran while one was open for 0% -> 0% of each run, Pallas kernels for 3% -> 3%
where the time goes in v5:
time: 92.5 us; the launch traced here: 92.1 us
  blocking collectives  75.1 us (81%)
  starting transfers between devices  8.69 us (9%)
  Pallas kernels  7.58 us (8%)
    all_to_all x4, blocking collectives, exchange(): return lax.all_to_all(x, 'ctx', 0, 0, tiled=True, axis_index_groups=devices)  56.9 us
    psum x1, blocking collectives, per_device(): gg = lax.psum(gg, 'dp')  18.2 us
    pallas_call x8, Pallas kernels, call(): pl.pallas_call(kernel, out_shape=shapes[0] if single else shapes, in_spec...  7.58 us
    all_to_all x1, starting transfers between devices, exchange(): return lax.all_to_all(x, 'ctx', 0, 0, tiled=True, axis_index_groups=devices)  6.01 us
    ppermute x1, starting transfers between devices, per_device(): got = lax.ppermute(mine, 'ctx', neighbour)  2.67 us
  transfers between devices with their start and end apart: 2, of which 0 were waited for; matrix products, arithmetic and copies ran while one was open for 0% of the time, Pallas kernels for 3%

profile of v5, /device:TPU:2, one launch (start us, length us, event | category | flops | bytes accessed | tf_op | source)
XLA Modules:
  0.0 92.1 jit_solution(11720613569823693129)
XLA Ops:
  0.6 1.7 %kv.1 = (f32[8,64,128]{2,1,0:T(8,128)S(1)}, bf16[128,1024]{1,0:T(8,128)(2,1)S(1)}, bf16[128,1024]{1,0:T(8,128)(2,1)S(1)}, f32[1,1024]{1,0:T(1,128)S(1)}) custom-call(bf16[128,1024]{1,0:T(8,128)(2,1)} %bitcast.20, bf16[128,1024]{1,0:T(8,128)(2,1)} %bitcast.21, f32[1,1024]{1,0:T(1,128)} %bitcast.22), custom_call_target="tpu_custom_call" | custom-call | flops 33554432 | bytes 1318912 | tf_op jit(solution)/shard_map/kv/pallas_call | solution.py:205
  2.4 13.9 %all_to_all.25.x_ref = f32[16,32,128]{2,1,0:T(8,128)S(1)} all-to-all(f32[16,32,128]{2,1,0:T(8,128)S(1)} %bitcast.19), channel_id=1, replica_groups={{0,1,2,3,4,5,6,7,8,9,10,11,12,13,14,15},{16,17,18,19,20,21,22,23,24,25,..., dimensions={0} | all-to-all | bytes 524288 | tf_op jit(solution)/shard_map/all_to_all | solution.py:226
  16.3 15.8 %all_to_all.26.z_ref = f32[4,32,128]{2,1,0:T(8,128)S(1)} all-to-all(f32[4,32,128]{2,1,0:T(8,128)S(1)} %totals.1), channel_id=1, replica_groups={{0,16,32,48},{1,17,33,49},{2,18,34,50},{3,19,35,51},{4,20,36,52},{5,21,..., dimensions={0} | all-to-all | bytes 131072 | tf_op jit(solution)/shard_map/all_to_all | solution.py:226
  32.1 0.0 copy-start
  32.1 0.0 copy-start.1
  32.1 10.4 %all_to_all.27 = f32[16,32,128]{2,1,0:T(8,128)S(1)} all-to-all(f32[16,32,128]{2,1,0:T(8,128)S(1)} %earlier.1), channel_id=1, replica_groups={{0,1,2,3,4,5,6,7,8,9,10,11,12,13,14,15},{16,17,18,19,20,21,22,23,24,25,..., dimensions={0} | all-to-all | bytes 524288 | tf_op jit(solution)/shard_map/all_to_all | solution.py:226
  42.6 0.0 copy-done
  42.6 0.0 copy-done.1
  42.6 1.5 %attn.1 = (f32[128,1024]{1,0:T(8,128)S(1)}, bf16[128,1024]{1,0:T(8,128)(2,1)S(1)}, f32[520,128]{1,0:T(8,128)S(1)}) custom-call(f32[8,64,128]{2,1,0:T(8,128)S(1)} %bitcast.13, bf16[128,1024]{1,0:T(8,128)(2,1)S(1)} %bitcast.15, bf16[128,1024]{1,0:T(8,128)(2,1)S(1)} %get-tuple-element.26.k_ref, bf16[128,1024]{1,0:T(8,128)(2,1)S(1)} %get-tuple-element.27.v_ref, ...), custom_call_target="tpu_custom_call" | custom-call | flops 201326592 | bytes 2367488 | tf_op jit(solution)/shard_map/attn/pallas_call | solution.py:205
  44.1 2.7 %collective-permute-start = (f32[520,128]{1,0:T(8,128)S(1)}, f32[520,128]{1,0:T(8,128)S(1)}, u32[]{:S(2)}, u32[]{:S(2)}) collective-permute-start(f32[520,128]{1,0:T(8,128)S(1)} %get-tuple-element.33.mine_ref), channel_id=1, source_target_pairs={{0,1},{1,0},{2,3},{3,2},{4,5},{5,4},{6,7},{7,6},{8,9},{9,8},{10,11... | collective-permute-start | bytes 798728 | tf_op jit(solution)/shard_map/ppermute | solution.py:264
  46.7 2.3 %local.1 = (bf16[128,1024]{1,0:T(8,128)(2,1)}, bf16[128,1024]{1,0:T(8,128)(2,1)}, f32[128,1024]{1,0:T(8,128)S(1)}, f32[128,1024]{1,0:T(8,128)S(1)}) custom-call(f32[8,64,128]{2,1,0:T(8,128)S(1)} %bitcast.14, bf16[128,1024]{1,0:T(8,128)(2,1)S(1)} %bitcast.16, bf16[128,1024]{1,0:T(8,128)(2,1)S(1)} %get-tuple-element.26.k_ref, ...), custom_call_target="tpu_custom_call" | custom-call | flops 335544320 | bytes 3411968 | tf_op jit(solution)/shard_map/local/pallas_call | solution.py:205
  49.1 0.0 collective-permute-done.got_ref
  49.1 16.8 %all_to_all.28.x_ref = f32[32,16,128]{2,1,0:T(8,128)S(1)} all-to-all(f32[32,16,128]{2,1,0:T(8,128)S(1)} %merge.1), channel_id=1, replica_groups={{0,2,4,6,8,10,12,14,16,18,20,22,24,26,28,30,32,34,36,38,40,42,44,46,48,..., dimensions={0} | all-to-all | bytes 524288 | tf_op jit(solution)/shard_map/all_to_all | solution.py:226
  65.9 0.7 later_sums.1
  66.7 6.0 %all-to-all-start.4 = ((f32[64,8,128]{2,1,0:T(8,128)}), f32[64,8,128]{2,1,0:T(8,128)S(1)}, u32[]{:S(2)}, u32[]{:S(2)}) async-start(f32[64,8,128]{2,1,0:T(8,128)} %get-tuple-element.37), calls=%async_computation.4 | async-start | bytes 524288 | tf_op jit(solution)/shard_map/all_to_all | solution.py:226
  72.7 18.2 %psum.7 = f32[8,128]{1,0:T(8,128)} all-reduce(f32[8,128]{1,0:T(8,128)S(1)} %get-tuple-element.38), channel_id=1, replica_groups=mesh['dp'=8,'ctx'=64] {'dp'}, use_global_device_ids=true, to_apply=%region_0.0 | all-reduce | flops 1024 | bytes 8192 | tf_op jit(solution)/shard_map/psum | solution.py:291
  90.9 0.0 all-to-all-done.4
  90.9 1.2 %later.1 = (bf16[128,1024]{1,0:T(8,128)(2,1)}, bf16[128,1024]{1,0:T(8,128)(2,1)}) custom-call(f32[32,2,8,128]{3,2,1,0:T(8,128)S(1)} %bitcast.17, f32[520,128]{1,0:T(8,128)S(1)} %collective-permute-done.got_ref, bf16[128,1024]{1,0:T(8,128)(2,1)S(1)} %get-tuple-element.26.k_ref, bf16[128,1024]{1,0:T(8,128)(2,1)S(1)} %get-tuple-element.27.v_ref, ...), custom_call_target="tpu_custom_call" | custom-call | flops 67108864 | bytes 2625536 | tf_op jit(solution)/shard_map/later/pallas_call | solution.py:205
  (3 shorter events, 0.1 us)
Async XLA Ops:
  32.1 10.5 %copy-start = (bf16[1,128,1024]{2,1,0:T(8,128)(2,1)S(1)}, bf16[1,128,1024]{2,1,0:T(8,128)(2,1)}, u32[]{:S(2)}) copy-start(bf16[1,128,1024]{2,1,0:T(8,128)(2,1)} %param.5) | copy-start | bytes 786436
  32.1 10.5 %copy-start.1 = (bf16[1,128,1024]{2,1,0:T(8,128)(2,1)S(1)}, bf16[1,128,1024]{2,1,0:T(8,128)(2,1)}, u32[]{:S(2)}) copy-start(bf16[1,128,1024]{2,1,0:T(8,128)(2,1)} %param.9) | copy-start | bytes 786436
  44.1 5.0 %collective-permute-start = (f32[520,128]{1,0:T(8,128)S(1)}, f32[520,128]{1,0:T(8,128)S(1)}, u32[]{:S(2)}, u32[]{:S(2)}) collective-permute-start(f32[520,128]{1,0:T(8,128)S(1)} %get-tuple-element.33.mine_ref), channel_id=1, source_target_pairs={{0,1},{1,0},{2,3},{3,2},{4,5},{5,4},{6,7},{7,6},{8,9},{9,8},{10,11... | collective-permute-start | bytes 798728 | tf_op jit(solution)/shard_map/ppermute | solution.py:264
  66.7 24.2 %all-to-all-start.4 = ((f32[64,8,128]{2,1,0:T(8,128)}), f32[64,8,128]{2,1,0:T(8,128)S(1)}, u32[]{:S(2)}, u32[]{:S(2)}) async-start(f32[64,8,128]{2,1,0:T(8,128)} %get-tuple-element.37), calls=%async_computation.4 | async-start | bytes 524288 | tf_op jit(solution)/shard_map/all_to_all | solution.py:226

commit v6 on v5

--- a/solution.py
+++ b/solution.py
@@ -244,7 +244,7 @@
             (k, v, gain),
             "kv",
             flops,
-            scratch=(pltpu.SemaphoreType.DMA((2, 4)), pltpu.SemaphoreType.DMA(())),
+            scratch=(pltpu.SemaphoreType.DMA((2, 2)), pltpu.SemaphoreType.DMA(())),
             far=True,
         )
         sent = exchange(kv.reshape(piece), inside)

time: 92.5 us -> 92.2 us (level)
  no operation moved by 1% of the time
where the time goes in v6:
time: 92.2 us; the launch traced here: 91.8 us
  blocking collectives  75.1 us (81%)
  starting transfers between devices  8.69 us (9%)
  Pallas kernels  7.28 us (8%)
    all_to_all x4, blocking collectives, exchange(): return lax.all_to_all(x, 'ctx', 0, 0, tiled=True, axis_index_groups=devices)  56.9 us
    psum x1, blocking collectives, per_device(): gg = lax.psum(gg, 'dp')  18.2 us
    pallas_call x8, Pallas kernels, call(): pl.pallas_call(kernel, out_shape=shapes[0] if single else shapes, in_spec...  7.28 us
    all_to_all x1, starting transfers between devices, exchange(): return lax.all_to_all(x, 'ctx', 0, 0, tiled=True, axis_index_groups=devices)  6.01 us
    ppermute x1, starting transfers between devices, per_device(): got = lax.ppermute(mine, 'ctx', neighbour)  2.67 us
  transfers between devices with their start and end apart: 2, of which 0 were waited for; matrix products, arithmetic and copies ran while one was open for 0% of the time, Pallas kernels for 3%

profile of v6, /device:TPU:2, one launch (start us, length us, event | category | flops | bytes accessed | tf_op | source)
XLA Modules:
  0.0 91.8 jit_solution(15044733056180163857)
XLA Ops:
  0.6 1.4 %kv.1 = (f32[8,64,128]{2,1,0:T(8,128)S(1)}, bf16[128,1024]{1,0:T(8,128)(2,1)S(1)}, bf16[128,1024]{1,0:T(8,128)(2,1)S(1)}, f32[1,1024]{1,0:T(1,128)S(1)}) custom-call(bf16[128,1024]{1,0:T(8,128)(2,1)} %bitcast.20, bf16[128,1024]{1,0:T(8,128)(2,1)} %bitcast.21, f32[1,1024]{1,0:T(1,128)} %bitcast.22), custom_call_target="tpu_custom_call" | custom-call | flops 33554432 | bytes 1318912 | tf_op jit(solution)/shard_map/kv/pallas_call | solution.py:205
  2.1 13.9 %all_to_all.25.x_ref = f32[16,32,128]{2,1,0:T(8,128)S(1)} all-to-all(f32[16,32,128]{2,1,0:T(8,128)S(1)} %bitcast.19), channel_id=1, replica_groups={{0,1,2,3,4,5,6,7,8,9,10,11,12,13,14,15},{16,17,18,19,20,21,22,23,24,25,..., dimensions={0} | all-to-all | bytes 524288 | tf_op jit(solution)/shard_map/all_to_all | solution.py:226
  16.0 15.8 %all_to_all.26.z_ref = f32[4,32,128]{2,1,0:T(8,128)S(1)} all-to-all(f32[4,32,128]{2,1,0:T(8,128)S(1)} %totals.1), channel_id=1, replica_groups={{0,16,32,48},{1,17,33,49},{2,18,34,50},{3,19,35,51},{4,20,36,52},{5,21,..., dimensions={0} | all-to-all | bytes 131072 | tf_op jit(solution)/shard_map/all_to_all | solution.py:226
  31.8 0.0 copy-start
  31.8 0.0 copy-start.1
  31.8 10.4 %all_to_all.27 = f32[16,32,128]{2,1,0:T(8,128)S(1)} all-to-all(f32[16,32,128]{2,1,0:T(8,128)S(1)} %earlier.1), channel_id=1, replica_groups={{0,1,2,3,4,5,6,7,8,9,10,11,12,13,14,15},{16,17,18,19,20,21,22,23,24,25,..., dimensions={0} | all-to-all | bytes 524288 | tf_op jit(solution)/shard_map/all_to_all | solution.py:226
  42.3 0.0 copy-done
  42.3 0.0 copy-done.1
  42.3 1.5 %attn.1 = (f32[128,1024]{1,0:T(8,128)S(1)}, bf16[128,1024]{1,0:T(8,128)(2,1)S(1)}, f32[520,128]{1,0:T(8,128)S(1)}) custom-call(f32[8,64,128]{2,1,0:T(8,128)S(1)} %bitcast.13, bf16[128,1024]{1,0:T(8,128)(2,1)S(1)} %bitcast.15, bf16[128,1024]{1,0:T(8,128)(2,1)S(1)} %get-tuple-element.26.k_ref, bf16[128,1024]{1,0:T(8,128)(2,1)S(1)} %get-tuple-element.27.v_ref, ...), custom_call_target="tpu_custom_call" | custom-call | flops 201326592 | bytes 2367488 | tf_op jit(solution)/shard_map/attn/pallas_call | solution.py:205
  43.8 2.7 %collective-permute-start = (f32[520,128]{1,0:T(8,128)S(1)}, f32[520,128]{1,0:T(8,128)S(1)}, u32[]{:S(2)}, u32[]{:S(2)}) collective-permute-start(f32[520,128]{1,0:T(8,128)S(1)} %get-tuple-element.33.mine_ref), channel_id=1, source_target_pairs={{0,1},{1,0},{2,3},{3,2},{4,5},{5,4},{6,7},{7,6},{8,9},{9,8},{10,11... | collective-permute-start | bytes 798728 | tf_op jit(solution)/shard_map/ppermute | solution.py:264
  46.4 2.3 %local.1 = (bf16[128,1024]{1,0:T(8,128)(2,1)}, bf16[128,1024]{1,0:T(8,128)(2,1)}, f32[128,1024]{1,0:T(8,128)S(1)}, f32[128,1024]{1,0:T(8,128)S(1)}) custom-call(f32[8,64,128]{2,1,0:T(8,128)S(1)} %bitcast.14, bf16[128,1024]{1,0:T(8,128)(2,1)S(1)} %bitcast.16, bf16[128,1024]{1,0:T(8,128)(2,1)S(1)} %get-tuple-element.26.k_ref, ...), custom_call_target="tpu_custom_call" | custom-call | flops 335544320 | bytes 3411968 | tf_op jit(solution)/shard_map/local/pallas_call | solution.py:205
  48.8 0.0 collective-permute-done.got_ref
  48.8 16.8 %all_to_all.28.x_ref = f32[32,16,128]{2,1,0:T(8,128)S(1)} all-to-all(f32[32,16,128]{2,1,0:T(8,128)S(1)} %merge.1), channel_id=1, replica_groups={{0,2,4,6,8,10,12,14,16,18,20,22,24,26,28,30,32,34,36,38,40,42,44,46,48,..., dimensions={0} | all-to-all | bytes 524288 | tf_op jit(solution)/shard_map/all_to_all | solution.py:226
  65.6 0.7 later_sums.1
  66.4 6.0 %all-to-all-start.4 = ((f32[64,8,128]{2,1,0:T(8,128)}), f32[64,8,128]{2,1,0:T(8,128)S(1)}, u32[]{:S(2)}, u32[]{:S(2)}) async-start(f32[64,8,128]{2,1,0:T(8,128)} %get-tuple-element.37), calls=%async_computation.4 | async-start | bytes 524288 | tf_op jit(solution)/shard_map/all_to_all | solution.py:226
  72.4 18.2 %psum.7 = f32[8,128]{1,0:T(8,128)} all-reduce(f32[8,128]{1,0:T(8,128)S(1)} %get-tuple-element.38), channel_id=1, replica_groups=mesh['dp'=8,'ctx'=64] {'dp'}, use_global_device_ids=true, to_apply=%region_0.0 | all-reduce | flops 1024 | bytes 8192 | tf_op jit(solution)/shard_map/psum | solution.py:291
  90.6 0.0 all-to-all-done.4
  90.6 1.2 %later.1 = (bf16[128,1024]{1,0:T(8,128)(2,1)}, bf16[128,1024]{1,0:T(8,128)(2,1)}) custom-call(f32[32,2,8,128]{3,2,1,0:T(8,128)S(1)} %bitcast.17, f32[520,128]{1,0:T(8,128)S(1)} %collective-permute-done.got_ref, bf16[128,1024]{1,0:T(8,128)(2,1)S(1)} %get-tuple-element.26.k_ref, bf16[128,1024]{1,0:T(8,128)(2,1)S(1)} %get-tuple-element.27.v_ref, ...), custom_call_target="tpu_custom_call" | custom-call | flops 67108864 | bytes 2625536 | tf_op jit(solution)/shard_map/later/pallas_call | solution.py:205
  (3 shorter events, 0.1 us)
Async XLA Ops:
  31.8 10.5 %copy-start = (bf16[1,128,1024]{2,1,0:T(8,128)(2,1)S(1)}, bf16[1,128,1024]{2,1,0:T(8,128)(2,1)}, u32[]{:S(2)}) copy-start(bf16[1,128,1024]{2,1,0:T(8,128)(2,1)} %param.5) | copy-start | bytes 786436
  31.8 10.5 %copy-start.1 = (bf16[1,128,1024]{2,1,0:T(8,128)(2,1)S(1)}, bf16[1,128,1024]{2,1,0:T(8,128)(2,1)}, u32[]{:S(2)}) copy-start(bf16[1,128,1024]{2,1,0:T(8,128)(2,1)} %param.9) | copy-start | bytes 786436
  43.8 5.0 %collective-permute-start = (f32[520,128]{1,0:T(8,128)S(1)}, f32[520,128]{1,0:T(8,128)S(1)}, u32[]{:S(2)}, u32[]{:S(2)}) collective-permute-start(f32[520,128]{1,0:T(8,128)S(1)} %get-tuple-element.33.mine_ref), channel_id=1, source_target_pairs={{0,1},{1,0},{2,3},{3,2},{4,5},{5,4},{6,7},{7,6},{8,9},{9,8},{10,11... | collective-permute-start | bytes 798728 | tf_op jit(solution)/shard_map/ppermute | solution.py:264
  66.4 24.2 %all-to-all-start.4 = ((f32[64,8,128]{2,1,0:T(8,128)}), f32[64,8,128]{2,1,0:T(8,128)S(1)}, u32[]{:S(2)}, u32[]{:S(2)}) async-start(f32[64,8,128]{2,1,0:T(8,128)} %get-tuple-element.37), calls=%async_computation.4 | async-start | bytes 524288 | tf_op jit(solution)/shard_map/all_to_all | solution.py:226
